TPU v7x, 128 devices: a whole 4x4x4 slice. The times are simulated.
128 devices in a mesh: depth: 8 (over x, z_lo), width: 2 (over z_hi), hidden: 8 (over y, core).
Axes of the slice: x: 4, y: 4, z: 4 (z_hi: 2, z_lo: 2; z = z_hi * 2 + z_lo), core: 2. Of those that a mesh axis runs over, the one named last changes fastest.
Arguments:
- inputs: float32 [8192, 3072], P('depth', 'width'), may hold values from -6 to 6
- weight: float32 [3072, 12288], P('width', ('hidden', 'depth')), may hold values from -0.3125 to 0.3125
- cotangent: float32 [8192, 12288], P('depth', 'hidden'), may hold values from -6 to 6
Outputs:
- input_grad: float32 [8192, 3072], P('depth', ('width', 'hidden'))
- weight_grad: float32 [3072, 12288], P('width', ('hidden', 'depth'))
All inputs are finite; a program needn't handle non-finite values.
Results may differ from a plain program's by a relative error of at most 0.00011.
Values sent between devices are 32-bit elements; how exact they have to be, the bound alone decides.
A program may use at most 192 MiB of HBM per device.

v0:
```python
import jax
import jax.numpy as jnp
from jax import lax
from jax.sharding import Mesh
from jax.sharding import PartitionSpec as P

DEPTH = ("depth_0", "depth_1")
HIDDEN_DEPTH = ("hidden", "depth_0", "depth_1")


inv_sqrt_two = 0.7071067811865476
inv_sqrt_two_pi = 0.3989422804014327


def cut_along(shard, dim, count):
    shape = shard.shape
    tiles = shard.reshape(*shape[:dim], count, shape[dim] // count, *shape[dim + 1 :])
    return jnp.moveaxis(tiles, dim, 0)


def sum_at_owner(shard, axis, dim):
    count = lax.axis_size(axis)
    tiles = lax.all_to_all(cut_along(shard, dim, count), axis, 0, 0, tiled=True)
    return jnp.sum(tiles, axis=0)


def sum_by_axis(so_far, axes):
    for axis in axes:
        so_far = lax.psum_scatter(so_far, axis, scatter_dimension=0, tiled=True)
    return so_far


def gelu_slope(preact):
    cumulative = 0.5 * (1.0 + jax.scipy.special.erf(preact * inv_sqrt_two))
    density = jnp.exp(-0.5 * preact * preact) * inv_sqrt_two_pi
    return cumulative + preact * density


def product(left, right):
    return jnp.dot(left, right, precision=lax.Precision.HIGHEST, preferred_element_type=jnp.float32)


def product_last(left, right):
    return lax.dot_general(
        left,
        right,
        (((1,), (1,)), ((), ())),
        precision=lax.Precision.HIGHEST,
        preferred_element_type=jnp.float32,
    )


def product_first(left, right):
    return lax.dot_general(
        left,
        right,
        (((0,), (0,)), ((), ())),
        precision=lax.Precision.HIGHEST,
        preferred_element_type=jnp.float32,
    )


def local(inputs, weight, cotangent):
    full_weight = lax.all_gather(weight, DEPTH, axis=1, tiled=True)
    partial_value = product(inputs, full_weight)
    shared_pre = sum_at_owner(partial_value, "width", 1)
    share_cols = shared_pre.shape[1]
    offset = lax.axis_index("width") * share_cols
    own_cotangent = lax.dynamic_slice_in_dim(cotangent, offset, share_cols, 1)
    pre_grad = lax.all_gather(own_cotangent * gelu_slope(shared_pre), "width", axis=1, tiled=True)
    input_part = product_last(pre_grad, full_weight)
    input_grad = lax.psum_scatter(input_part, "hidden", scatter_dimension=1, tiled=True)
    weight_rows = sum_by_axis(product_first(pre_grad, inputs), DEPTH)
    return (input_grad, weight_rows.T)


def solution(mesh):
    torus = Mesh(
        mesh.devices.reshape(4, 2, mesh.shape["width"], mesh.shape["hidden"]),
        ("depth_0", "depth_1", "width", "hidden"),
    )
    in_specs = (P(DEPTH, "width"), P("width", HIDDEN_DEPTH), P(DEPTH, "hidden"))
    out_specs = (P(DEPTH, ("width", "hidden")), P("width", HIDDEN_DEPTH))
    return jax.shard_map(local, mesh=torus, in_specs=in_specs, out_specs=out_specs, check_vma=False)
```

profile of v0, /device:TPU:32, one launch (start us, length us, event | category | flops | bytes accessed | tf_op | source)
XLA Modules:
  0.0 625.3 jit_solution(14935465865608592660)
XLA Ops:
  7.2 0.0 all-gather.3.cloned.1.call-start
  7.2 0.7 all-gather.3.cloned.1.call-update
  7.9 190.6 %all-gather.3.cloned.1.call-done = f32[1536,1536]{0,1:T(8,128)} async-done(((f32[1536,192]{0,1:T(8,128)}), f32[1536,1536]{0,1:T(8,128)}) %all-gather.3.cloned.1.call-update) | async-done | bytes 9437200 | tf_op jit(solution)/shard_map/all_gather | solution.py:64
  198.5 34.9 %fusion.5 = f32[1024,1536]{1,0:T(8,128)S(1)} fusion(f32[1024,1536]{1,0:T(8,128)} %param.3, f32[1536,1536]{0,1:T(8,128)} %all-gather.3.cloned.1.call-done), kind=kOutput, calls=%fused_computation.7 | convolution fusion | flops 28991029248 | bytes 22020096 | tf_op jit(solution)/shard_map/dot_general | solution.py:40
  233.4 3.0 copy.8
  236.4 6.3 %all-to-all-start = ((f32[2,1024,768]{2,1,0:T(8,128)}), f32[2,1024,768]{2,1,0:T(8,128)}, u32[]{:S(2)}, u32[]{:S(2)}) async-start(f32[2,1024,768]{2,1,0:T(8,128)} %bitcast.14), calls=%async_computation | async-start | bytes 12582912 | tf_op jit(solution)/shard_map/all_to_all | solution.py:23
  242.7 0.2 all-gather.5.cloned.1.call-start
  242.9 71.3 %all-to-all-done = f32[2,1024,768]{2,1,0:T(8,128)} async-done(((f32[2,1024,768]{2,1,0:T(8,128)}), f32[2,1024,768]{2,1,0:T(8,128)}, u32[]{:S(2)}, u32[]{:S(2)}) %all-to-all-start) | async-done | bytes 6291488 | tf_op jit(solution)/shard_map/all_to_all | solution.py:23
  314.2 3.6 reduce_sum.9
  317.7 3.8 fusion.4
  321.6 0.0 all-gather.5.cloned.1.call-update
  321.6 0.0 reduce-scatter.6.cloned.1.call-start
  321.6 88.5 %all-gather.5.cloned.1.call-done = f32[1024,1536]{1,0:T(8,128)} async-done(((f32[1024,768]{1,0:T(8,128)}), f32[1024,1536]{1,0:T(8,128)}) %all-gather.5.cloned.1.call-update) | async-done | bytes 6291472 | tf_op jit(solution)/shard_map/all_gather | solution.py:70
  410.1 35.7 %fusion.7 = f32[1536,1536]{1,0:T(8,128)} fusion(f32[1024,1536]{1,0:T(8,128)} %all-gather.5.cloned.1.call-done, f32[1024,1536]{1,0:T(8,128)} %param.3), kind=kOutput, calls=%fused_computation.9 | convolution fusion | flops 28991029248 | bytes 22020096 | tf_op jit(solution)/shard_map/dot_general | solution.py:54
  445.9 0.0 reduce-scatter.6.cloned.1.call-update
  445.9 0.3 reduce-scatter.4.cloned.1.call-start
  446.2 34.7 %fusion.6 = f32[1024,1536]{0,1:T(8,128)} fusion(f32[1024,1536]{1,0:T(8,128)} %all-gather.5.cloned.1.call-done, f32[1536,1536]{0,1:T(8,128)} %all-gather.3.cloned.1.call-done), kind=kOutput, calls=%fused_computation.8 | convolution fusion | flops 28991029248 | bytes 22020096 | tf_op jit(solution)/shard_map/dot_general | solution.py:44
  480.9 0.0 reduce-scatter.4.cloned.1.call-update
  480.9 0.0 reduce-scatter.8.cloned.1.call-start
  481.0 54.1 %reduce-scatter.6.cloned.1.call-done = f32[384,1536]{1,0:T(8,128)} async-done(((f32[1536,1536]{1,0:T(8,128)}), f32[384,1536]{1,0:T(8,128)}) %reduce-scatter.6.cloned.1.call-update) | async-done | bytes 2359312 | tf_op jit(solution)/shard_map/reduce_scatter | solution.py:29
  535.1 0.0 reduce-scatter.8.cloned.1.call-update
  535.1 45.1 %reduce-scatter.4.cloned.1.call-done = f32[1024,192]{0,1:T(8,128)} async-done(((f32[1024,1536]{0,1:T(8,128)}), f32[1024,192]{0,1:T(8,128)}) %reduce-scatter.4.cloned.1.call-update) | async-done | bytes 786448 | tf_op jit(solution)/shard_map/reduce_scatter | solution.py:72
  580.2 38.5 %reduce-scatter.8.cloned.1.call-done = f32[192,1536]{1,0:T(8,128)} async-done(((f32[384,1536]{1,0:T(8,128)}), f32[192,1536]{1,0:T(8,128)}) %reduce-scatter.8.cloned.1.call-update) | async-done | bytes 1179664 | tf_op jit(solution)/shard_map/reduce_scatter | solution.py:29
Async XLA Ops:
  7.2 191.3 %all-gather.3.cloned.1.call-start = ((), (), s32[]{:S(2)}) async-start(), calls=%async_computation.4 | async-start | bytes 10616832 | tf_op jit(solution)/shard_map/all_gather | solution.py:64
  236.4 77.8 %all-to-all-start = ((f32[2,1024,768]{2,1,0:T(8,128)}), f32[2,1024,768]{2,1,0:T(8,128)}, u32[]{:S(2)}, u32[]{:S(2)}) async-start(f32[2,1024,768]{2,1,0:T(8,128)} %bitcast.14), calls=%async_computation | async-start | bytes 12582912 | tf_op jit(solution)/shard_map/all_to_all | solution.py:23
  242.7 167.4 %all-gather.5.cloned.1.call-start = ((), (), s32[]{:S(2)}) async-start(), calls=%async_computation.5 | async-start | bytes 9437184 | tf_op jit(solution)/shard_map/all_gather | solution.py:70
  321.6 213.5 %reduce-scatter.6.cloned.1.call-start = ((), (), s32[]{:S(2)}) async-start(), calls=%async_computation.7 | async-start | bytes 11796480 | tf_op jit(solution)/shard_map/reduce_scatter | solution.py:29
  445.9 134.3 %reduce-scatter.4.cloned.1.call-start = ((), (), s32[]{:S(2)}) async-start(), calls=%async_computation.6 | async-start | bytes 7077888 | tf_op jit(solution)/shard_map/reduce_scatter | solution.py:72
  480.9 137.8 %reduce-scatter.8.cloned.1.call-start = ((), (), s32[]{:S(2)}) async-start(), calls=%async_computation.8 | async-start | bytes 3538944 | tf_op jit(solution)/shard_map/reduce_scatter | solution.py:29
Sparse Core Ops, SparseCore 0:
  9.6 188.7 all-gather.2
  321.7 88.3 all-gather.4
  446.0 89.0 reduce-scatter.5
  537.9 42.2 reduce-scatter.3
  583.0 35.6 reduce-scatter.7
where the time goes:
time: 628 us; the launch traced here: 625 us
  waiting for transfers between devices  489 us (78%)
  matrix products  105 us (17%)
  between operations  13.8 us (2%)
  other arithmetic  7.38 us (1%)
  starting transfers between devices  6.88 us (1%)
    all_gather x1, waiting for transfers between devices, local(): full_weight = lax.all_gather(weight, DEPTH, axis=1, tiled=True)  191 us
    reduce_scatter x2, waiting for transfers between devices, sum_by_axis(): so_far = lax.psum_scatter(so_far, axis, scatter_dimension=0, tiled=True)  92.6 us
    all_gather x1, waiting for transfers between devices, local(): lax.all_gather(own_cotangent * gelu_slope(shared_pre), 'width', axis=1, t...  88.5 us
    all_to_all x1, waiting for transfers between devices, sum_at_owner(): tiles = lax.all_to_all(cut_along(shard, dim, count), axis, 0, 0, tiled=True)  71.3 us
    reduce_scatter x1, waiting for transfers between devices, local(): lax.psum_scatter(input_part, 'hidden', scatter_dimension=1, tiled=True)  45.1 us
    dot_general x1, matrix products, product_first(): lax.dot_general(left, right, (((0,), (0,)), ((), ())), precision=lax.Prec...  35.7 us
    dot_general x1, matrix products, product(): jnp.dot(left, right, precision=lax.Precision.HIGHEST, preferred_element_t...  34.9 us
    dot_general x1, matrix products, product_last(): lax.dot_general(left, right, (((1,), (1,)), ((), ())), precision=lax.Prec...  34.7 us
  transfers between devices with their start and end apart: 6, of which 6 were waited for; matrix products, arithmetic and copies ran while one was open for 6% of the time, Pallas kernels for 0%

commit v1 on v0

v1 whole, which is shorter than its diff:
```python
import jax
import jax.numpy as jnp
from jax import lax
from jax.experimental import pallas as pl
from jax.experimental.pallas import tpu as pltpu
from jax.sharding import Mesh
from jax.sharding import PartitionSpec as P

AXES = ("x", "zl", "zh", "y", "c")
MESH = pl.DeviceIdType.MESH
PIECES = 3

inv_sqrt_two = 0.7071067811865476
inv_sqrt_two_pi = 0.3989422804014327


class Place:
    def __init__(self):
        self.x, self.zl, self.zh, self.y, self.c = (lax.axis_index(a) for a in AXES)
        self.z = 2 * self.zh + self.zl
        self.inner = self.zl != self.zh
        self.outer = self.zl == self.zh
        self.to_inner = self.z + 1 - 2 * self.zh
        self.to_outer = 3 * self.zh

    def at_z(self, z):
        return (self.x, lax.rem(z, 2), lax.div(z, 2), self.y, self.c)

    def step(self, dx=0, dy=0, dz=0, dc=0):
        z = lax.rem(self.z + dz + 4, 4)
        return (
            lax.rem(self.x + dx + 4, 4),
            lax.rem(z, 2),
            lax.div(z, 2),
            lax.rem(self.y + dy + 4, 4),
            lax.rem(self.c + dc, 2),
        )


def enter(me):
    barrier = pltpu.get_barrier_semaphore()
    steps = [
        dict(dx=1), dict(dx=-1), dict(dy=1), dict(dy=-1),
        dict(dz=1), dict(dz=-1), dict(dz=2), dict(dc=1),
    ]
    for step in steps:
        pl.semaphore_signal(barrier, inc=1, device_id=me.step(**step), device_id_type=MESH)
    pl.semaphore_wait(barrier, len(steps))


def remote(src, dst, send, recv, device):
    return pltpu.make_async_remote_copy(
        src_ref=src, dst_ref=dst, send_sem=send, recv_sem=recv, device_id=device, device_id_type=MESH
    )


def gather_kernel(xh, wt, xo, wf, zs, zr, fs, xs, xr, gs, gr, s1, r1, sy, ry, sf, rf, sc, rc):
    me = Place()
    rows = wt.shape[0] // PIECES
    tok = xh.shape[0] // 8
    half = tok // 2

    def piece(p):
        return pl.ds(p * rows, rows)

    enter(me)
    slot = me.inner.astype(jnp.int32)
    for p in range(PIECES):
        remote(wt.at[piece(p)], wf.at[me.x, slot, piece(p)], zs.at[p], zr.at[slot, p], me.at_z(me.to_inner)).start()

        @pl.when(me.outer)
        def _():
            pltpu.make_async_copy(wt.at[piece(p)], wf.at[me.x, 0, piece(p)], zr.at[0, p]).start()

    def part(y, c):
        return pl.ds((y * 2 + c) * tok, tok)

    mine = part(me.y, me.c)
    first = remote(xh.at[mine], xo.at[mine], s1, r1, me.step(dz=2))
    first.start()

    for k in range(2 * PIECES):
        s = jnp.where(me.inner, k % 2, k // PIECES)
        p = jnp.where(me.inner, k // 2, k % PIECES)
        here = wf.at[me.x, s, piece(p)]
        pltpu.make_async_copy(here, here, zr.at[s, p]).wait()

        @pl.when(me.inner & (s == 1))
        def _():
            remote(here, here, fs.at[p], zr.at[s, p], me.at_z(me.to_outer)).start()

        for d, dx in enumerate((1, -1)):
            remote(here, here, xs.at[d, s, p], xr.at[d, s, p], me.step(dx=dx)).start()

    first.wait()
    across = [remote(xo.at[mine], xo.at[mine], sy.at[d], ry.at[d], me.step(dy=dy)) for d, dy in enumerate((1, -1))]
    for copy in across:
        copy.start()
    shares = [remote(xo.at[mine], xo.at[mine], sc.at[0], rc.at[0], me.step(dc=1))]
    shares[0].start()

    def pass_on(p):
        for d, dx in enumerate((1, -1)):
            there = wf.at[lax.rem(me.x - dx + 4, 4), d, piece(p)]
            remote(there, there, gs.at[d, p], xr.at[d, d, p], me.step(dx=dx)).wait_recv()
            remote(there, there, gs.at[d, p], gr.at[d, p], me.step(dx=dx)).start()

    pass_on(0)
    halves = []
    for d, dy in enumerate((1, -1)):
        across[d].wait_recv()
        from_y = lax.rem(me.y - dy + 4, 4)
        rows_of = pl.ds((from_y * 2 + me.c) * tok + d * half, half)
        halves.append(remote(xo.at[rows_of], xo.at[rows_of], sf.at[d], rf.at[d], me.step(dy=dy)))
        halves[-1].start()
        whole = part(from_y, me.c)
        shares.append(remote(xo.at[whole], xo.at[whole], sc.at[1 + d], rc.at[1 + d], me.step(dc=1)))
        shares[-1].start()
    for p in range(1, PIECES):
        pass_on(p)
    far = part(lax.rem(me.y + 2, 4), me.c)
    for d in range(2):
        halves[d].wait_recv()
    shares.append(remote(xo.at[far], xo.at[far], sc.at[3], rc.at[3], me.step(dc=1)))
    shares[-1].start()

    for p in range(PIECES):
        remote(wt.at[piece(p)], wt.at[piece(p)], zs.at[p], zs.at[p], me.step(dc=1)).wait_send()

        @pl.when(me.inner)
        def _():
            remote(wt.at[piece(p)], wt.at[piece(p)], fs.at[p], fs.at[p], me.step(dc=1)).wait_send()

        for d in range(2):
            for s in range(2):
                copy = remote(wt.at[piece(p)], wt.at[piece(p)], xs.at[d, s, p], xr.at[d, s, p], me.step(dc=1))
                copy.wait_send()
                if s != d:
                    copy.wait_recv()
            remote(wt.at[piece(p)], wt.at[piece(p)], gs.at[d, p], gr.at[d, p], me.step(dc=1)).wait()
    for d in range(2):
        across[d].wait_send()
        halves[d].wait_send()
    for copy in shares:
        copy.wait()


def gather(inputs, wt):
    dma = pltpu.SemaphoreType.DMA
    any_space = pl.BlockSpec(memory_space=pltpu.HBM)
    return pl.pallas_call(
        gather_kernel,
        out_shape=(
            jax.ShapeDtypeStruct(inputs.shape, jnp.float32),
            jax.ShapeDtypeStruct((4, 2) + wt.shape, jnp.float32),
        ),
        in_specs=[any_space, any_space],
        out_specs=(any_space, any_space),
        scratch_shapes=[
            dma((PIECES,)), dma((2, PIECES)), dma((PIECES,)),
            dma((2, 2, PIECES)), dma((2, 2, PIECES)),
            dma((2, PIECES)), dma((2, PIECES)),
            dma, dma, dma((2,)), dma((2,)), dma((2,)), dma((2,)), dma((4,)), dma((4,)),
        ],
        compiler_params=pltpu.CompilerParams(collective_id=0, has_side_effects=True),
    )(inputs, wt)


def reduce_kernel(
    dw, dx, wout, xout, far, near, v, zin, zsum, cin, acc, yfar, ynear, xz,
    fs, fr, ns, nr, zs, zr, os_, cs, cr, yfs, yfr, yns, ynr, s1, r1,
):
    me = Place()
    rows = wout.shape[0] // PIECES

    def piece(p):
        return pl.ds(p * rows, rows)

    def x_at(d):
        return lax.rem(me.x + d + 4, 4)

    def y_at(d):
        return lax.rem(me.y + d + 4, 4)

    enter(me)
    dirs = ((0, 1), (1, -1))
    opposite = []
    straight = []
    for p in range(PIECES):
        for d, step in dirs:
            copy = remote(dw.at[x_at(2), d, piece(p)], far.at[d, piece(p)], fs.at[d, p], fr.at[d, p], me.step(dx=step))
            copy.start()
            opposite.append(copy)
    shares = []
    for i, (s, dy) in enumerate(((0, 2), (1, 2), (0, 1), (1, -1), (1, 1), (0, -1), (0, 0), (1, 0))):
        copy = remote(dx.at[s, y_at(dy), 1 - me.c], cin.at[s, y_at(dy)], cs.at[i], cr.at[i], me.step(dc=1))
        copy.start()
        shares.append((copy, s, dy))
    for p in range(PIECES):
        for d, step in dirs:
            copy = remote(
                dw.at[x_at(step), 1 - d, piece(p)], near.at[d, 1 - d, piece(p)],
                ns.at[d, 1 - d, p], nr.at[d, 1 - d, p], me.step(dx=step),
            )
            copy.start()
            straight.append(copy)

    def on_chip(i):
        copy, s, dy = shares[i]
        copy.wait_recv()
        acc[s, y_at(dy)] = dx[s, y_at(dy), me.c] + cin[s, y_at(dy)]

    y_copies = []
    for d, step in dirs:
        on_chip(d)
        copy = remote(acc.at[d, y_at(2)], yfar.at[d], yfs.at[d], yfr.at[d], me.step(dy=step))
        copy.start()
        y_copies.append(copy)
    for i in range(2, 6):
        on_chip(i)
    for d, step in dirs:
        copy = remote(
            acc.at[1 - d, y_at(step)], ynear.at[d, 1 - d], yns.at[d, 1 - d], ynr.at[d, 1 - d], me.step(dy=step)
        )
        copy.start()
        y_copies.append(copy)
    for i in range(6, 8):
        on_chip(i)

    def pass_on(p):
        for d, step in dirs:
            opposite[2 * p + d].wait_recv()
            far[d, piece(p)] = far[d, piece(p)] + dw[x_at(step), d, piece(p)]
            copy = remote(
                far.at[d, piece(p)], near.at[d, d, piece(p)], ns.at[d, d, p], nr.at[d, d, p], me.step(dx=step)
            )
            copy.start()
            straight.append(copy)

    pass_on(0)
    pass_on(1)
    for d, step in dirs:
        y_copies[d].wait_recv()
        yfar[d] = yfar[d] + acc[d, y_at(step)]
        copy = remote(yfar.at[d], ynear.at[d, d], yns.at[d, d], ynr.at[d, d], me.step(dy=step))
        copy.start()
        y_copies.append(copy)
    pass_on(2)

    for d in range(2):
        y_copies[2 + d].wait_recv()
        y_copies[4 + d].wait_recv()
    acc[1, me.y] = acc[1, me.y] + ynear[0, 1] + ynear[1, 1]
    last = remote(acc.at[1, me.y], xz, s1, r1, me.step(dz=2))
    last.start()

    z_copies = []
    outs = []
    for p in range(PIECES):
        for d in range(2):
            straight[2 * p + d].wait_recv()
            straight[2 * PIECES + 2 * p + d].wait_recv()
        for s in range(2):
            v[s, piece(p)] = dw[me.x, s, piece(p)] + near[0, s, piece(p)] + near[1, s, piece(p)]

        @pl.when(me.outer)
        def _():
            remote(v.at[1, piece(p)], zin.at[0, piece(p)], zs.at[p], zr.at[0, p], me.at_z(me.to_inner)).start()

        @pl.when(me.inner)
        def _():
            remote(v.at[0, piece(p)], zin.at[1, piece(p)], zs.at[p], zr.at[1, p], me.at_z(me.to_outer)).start()

    for p in range(PIECES):
        @pl.when(me.inner)
        def _():
            remote(v.at[1, piece(p)], zin.at[0, piece(p)], os_.at[p], zr.at[0, p], me.at_z(me.to_inner)).wait_recv()
            zsum[piece(p)] = v[1, piece(p)] + zin[0, piece(p)]
            remote(zsum.at[piece(p)], zin.at[1, piece(p)], os_.at[p], zr.at[1, p], me.at_z(me.to_inner)).start()

    xout[...] = acc[0, me.y] + ynear[0, 0] + ynear[1, 0]
    last.wait_recv()
    xout[...] = xout[...] + xz[...]
    for p in range(PIECES):
        remote(v.at[1, piece(p)], zin.at[1, piece(p)], zs.at[p], zr.at[1, p], me.step(dz=1)).wait_recv()
        wout[piece(p)] = jnp.where(me.outer, v[0, piece(p)] + zin[1, piece(p)], zin[1, piece(p)])

    for p in range(PIECES):
        remote(v.at[1, piece(p)], zin.at[1, piece(p)], zs.at[p], zr.at[1, p], me.step(dz=1)).wait_send()

        @pl.when(me.inner)
        def _():
            remote(v.at[1, piece(p)], zin.at[0, piece(p)], os_.at[p], zr.at[0, p], me.step(dz=1)).wait_send()

    for copy in opposite + straight + y_copies + [s[0] for s in shares] + [last]:
        copy.wait_send()


def reduce(dw, dx):
    dma = pltpu.SemaphoreType.DMA
    vmem = pltpu.VMEM
    f32 = jnp.float32
    _, _, r, d = dw.shape
    _, _, _, b, t = dx.shape
    spec = pl.BlockSpec(memory_space=pltpu.VMEM)
    return pl.pallas_call(
        reduce_kernel,
        out_shape=(jax.ShapeDtypeStruct((r, d), f32), jax.ShapeDtypeStruct((b, t), f32)),
        in_specs=[spec, spec],
        out_specs=(spec, spec),
        scratch_shapes=[
            vmem((2, r, d), f32), vmem((2, 2, r, d), f32), vmem((2, r, d), f32), vmem((2, r, d), f32), vmem((r, d), f32),
            vmem((2, 4, b, t), f32), vmem((2, 4, b, t), f32), vmem((2, b, t), f32), vmem((2, 2, b, t), f32), vmem((b, t), f32),
            dma((2, PIECES)), dma((2, PIECES)), dma((2, 2, PIECES)), dma((2, 2, PIECES)),
            dma((PIECES,)), dma((2, PIECES)), dma((PIECES,)),
            dma((8,)), dma((8,)), dma((2,)), dma((2,)), dma((2, 2)), dma((2, 2)), dma, dma,
        ],
        compiler_params=pltpu.CompilerParams(collective_id=1, has_side_effects=True, vmem_limit_bytes=60 << 20),
    )(dw, dx)


def gelu_slope(preact):
    cumulative = 0.5 * (1.0 + jax.scipy.special.erf(preact * inv_sqrt_two))
    density = jnp.exp(-0.5 * preact * preact) * inv_sqrt_two_pi
    return cumulative + preact * density


def product(left, right, left_dim, right_dim):
    return lax.dot_general(
        left, right, (((left_dim,), (right_dim,)), ((), ())),
        precision=lax.Precision.HIGH, preferred_element_type=jnp.float32,
    )


def local(inputs, weight, cotangent):
    wt = weight.T
    r, d = wt.shape
    tok = inputs.shape[0]
    other, wf = gather(inputs, wt)
    near = wf[:, 0].reshape(4 * r, d)
    far = wf[:, 1].reshape(4 * r, d)
    cot = cotangent.reshape(tok, 4, 2, r)
    own = lax.dynamic_index_in_dim(cot, lax.axis_index("zh"), 2, keepdims=False).reshape(tok, 4 * r)
    preact = product(inputs, near, 1, 1) + product(other, far, 1, 1)
    pre_grad = own * gelu_slope(preact)
    dw = jnp.stack([product(pre_grad, half, 0, 0).reshape(4, r, d) for half in (inputs, other)], axis=1)
    dx = jnp.stack([product(half, pre_grad, 0, 1).reshape(4, 2, d // 8, tok) for half in (near, far)], axis=0)
    wout, xout = reduce(dw, dx)
    return (xout.T, wout.T)


def solution(mesh):
    torus = Mesh(mesh.devices.reshape(4, 2, 2, 4, 2), AXES)
    in_specs = (P(("x", "zl"), "zh"), P("zh", ("y", "c", "x", "zl")), P(("x", "zl"), ("y", "c")))
    out_specs = (P(("x", "zl"), ("zh", "y", "c")), P("zh", ("y", "c", "x", "zl")))
    return jax.shard_map(local, mesh=torus, in_specs=in_specs, out_specs=out_specs, check_vma=False)
```

time: 628 us -> 339 us (0.54)
  waiting for transfers between devices: 489 us -> 0 us
  Pallas kernels: 0 us -> 224 us
  matrix products: 105 us -> 64.4 us
  local copies, waits for them, and re-layouts: 3.02 us -> 30.3 us
  between operations: 13.8 us -> 1.03 us
  starting transfers between devices: 6.88 us -> 0 us
  other arithmetic: 7.38 us -> 13.8 us
    all_gather x2 -> x0, waiting for transfers between devices: 279 us -> none  [the longest x1 191 us: local(): full_weight = lax.all_gather(weight, DEPTH, axis=1, tiled=True)]
    pallas_call x0 -> x2, Pallas kernels: none -> 224 us  [the longest x1 131 us: reduce(): pl.pallas_call(reduce_kernel, out_shape=(jax.ShapeDtypeStruct((r, d), f32...]
    reduce_scatter x3 -> x0, waiting for transfers between devices: 138 us -> none  [the longest x2 92.6 us: sum_by_axis(): so_far = lax.psum_scatter(so_far, axis, scatter_dimension=0, tiled=True)]
    all_to_all x1 -> x0, waiting for transfers between devices: 71.3 us -> none  [sum_at_owner(): tiles = lax.all_to_all(cut_along(shard, dim, count), axis, 0, 0, tiled=True)]
    dot_general x3 -> x6, matrix products: 105 us -> 64.4 us  [product(): lax.dot_general(left, right, (((left_dim,), (right_dim,)), ((), ())), pre...]
    another operation x0 -> x2, other arithmetic: none -> 13.8 us  [the longest x1 9.37 us: local(): jnp.stack([product(half, pre_grad, 0, 1).reshape(4, 2, d // 8, tok) for h...]
    dot_general x0 -> x2, local copies, waits for them, and re-layouts: none -> 12.4 us  [product(): lax.dot_general(left, right, (((left_dim,), (right_dim,)), ((), ())), pre...]
    unnamed x0 -> x21, local copies, waits for them, and re-layouts: none -> 11.1 us
  transfers between devices with their start and end apart: 6 -> 0, of which waited for: 6 -> 0; matrix products, arithmetic and copies ran while one was open for 6% -> 0% of each run, Pallas kernels for 0% -> 0%
where the time goes in v1:
time: 339 us; the launch traced here: 334 us
  Pallas kernels  224 us (66%)
  matrix products  64.4 us (19%)
  local copies, waits for them, and re-layouts  30.3 us (9%)
  other arithmetic  13.8 us (4%)
    pallas_call x1, Pallas kernels, reduce(): pl.pallas_call(reduce_kernel, out_shape=(jax.ShapeDtypeStruct((r, d), f32...  131 us
    pallas_call x1, Pallas kernels, gather(): pl.pallas_call(gather_kernel, out_shape=(jax.ShapeDtypeStruct(inputs.shap...  92.8 us
    dot_general x6, matrix products, product(): lax.dot_general(left, right, (((left_dim,), (right_dim,)), ((), ())), pre...  64.4 us
    dot_general x2, local copies, waits for them, and re-layouts, product(): lax.dot_general(left, right, (((left_dim,), (right_dim,)), ((), ())), pre...  12.4 us
    unnamed x21, local copies, waits for them, and re-layouts  11.1 us
    another operation x1, other arithmetic, local(): jnp.stack([product(half, pre_grad, 0, 1).reshape(4, 2, d // 8, tok) for h...  9.37 us

profile of v1, /device:TPU:32, one launch (start us, length us, event | category | flops | bytes accessed | tf_op | source)
XLA Modules:
  0.0 333.5 jit_solution(511078223680610472)
XLA Ops:
  0.6 6.6 %copy.11 = f32[1024,1536]{0,1:T(8,128)} copy(f32[1024,1536]{1,0:T(8,128)} %param.5) | data formatting | bytes 12582912 | tf_op args[2]
  7.2 2.1 constant_dynamic-slice_fusion
  9.3 92.8 %shard_map.50 = (f32[1024,1536]{1,0:T(8,128)}, f32[4,2,192,1536]{3,2,1,0:T(8,128)}) custom-call(f32[1024,1536]{1,0:T(8,128)} %xh.1, f32[192,1536]{1,0:T(8,128)} %bitcast.57), custom_call_target="tpu_custom_call" | custom-call | tf_op jit(solution)/shard_map/pallas_call | solution.py:151
  102.1 0.0 slice-start
  102.1 4.8 %fusion.15 = (f32[4,1,192,1536]{3,2,1,0:T(8,128)S(1)}, f32[4,1,192,1536]{3,2,1,0:T(8,128)S(1)}) fusion(f32[4,2,192,1536]{3,2,1,0:T(8,128)} %get-tuple-element.6), kind=kLoop, calls=%fused_computation.16 | loop fusion | bytes 18874368 | tf_op jit(solution)/shard_map/slice | solution.py:340
  106.9 0.0 copy-start
  106.9 0.0 copy-start.1
  106.9 0.0 slice-start.1
  107.0 14.0 %fusion.16 = f32[1024,768]{0,1:T(8,128)} fusion(f32[1024,1536]{1,0:T(8,128)} %get-tuple-element.7, f32[768,1536]{1,0:T(8,128)S(1)} %bitcast.46), kind=kOutput, calls=%fused_computation.17 | convolution fusion | flops 7247757312 | bytes 14155776 | tf_op jit(solution)/shard_map/dot_general | solution.py:329
  121.0 0.0 copy-done
  121.0 0.0 copy-done.1
  121.0 0.0 slice-done
  121.0 0.0 slice-done.1
  121.0 0.0 copy-start.2
  121.0 10.8 %fusion.4 = f32[1024,768]{0,1:T(8,128)S(1)} fusion(f32[1024,4,1,192]{0,3,2,1:T(8,128)S(1)} %constant_dynamic-slice_fusion, f32[1024,768]{0,1:T(8,128)} %fusion.16, f32[768,1536]{1,0:T(8,128)S(1)} %bitcast.44, f32[1024,1536]{1,0:T(8,128)S(1)} %bitcast.50), kind=kOutput, calls=%fused_computation.7 | convolution fusion | flops 7255621632 | bytes 20447232 | tf_op jit(solution)/shard_map/dot_general | solution.py:329
  131.8 0.0 copy-done.2
  131.8 0.0 copy-start.3
  131.8 8.2 %fusion.18 = f32[768,1536]{1,0:T(8,128)S(1)} fusion(f32[1024,768]{0,1:T(8,128)S(1)} %fusion.4, f32[1024,1536]{1,0:T(8,128)S(1)} %copy-done.2), kind=kOutput, calls=%fused_computation.19 | convolution fusion | flops 7247757312 | bytes 14155776 | tf_op jit(solution)/shard_map/dot_general | solution.py:329
  140.0 0.0 copy-done.3
  140.0 7.9 %fusion.17 = f32[768,1536]{1,0:T(8,128)S(1)} fusion(f32[1024,768]{0,1:T(8,128)S(1)} %fusion.4, f32[1024,1536]{1,0:T(8,128)S(1)} %bitcast.50), kind=kOutput, calls=%fused_computation.18 | convolution fusion | flops 7247757312 | bytes 14155776 | tf_op jit(solution)/shard_map/dot_general | solution.py:329
  148.0 4.4 %pad_maximum_fusion.1.dw = f32[4,2,192,1536]{3,2,1,0:T(8,128)} fusion(f32[4,1,192,1536]{3,2,1,0:T(8,128)S(1)} %bitcast.55, f32[4,1,192,1536]{3,2,1,0:T(8,128)S(1)} %bitcast.56), kind=kLoop, calls=%fused_computation.1 | loop fusion | flops 2359296 | bytes 18874368 | tf_op jit(solution)/shard_map/stack | solution.py:346
  152.4 0.0 copy-start.4
  152.4 6.2 %copy.15 = f32[1536,768]{1,0:T(8,128)} copy(f32[1536,768]{0,1:T(8,128)} %bitcast.47) | data formatting | bytes 9437184 | tf_op jit(solution)/shard_map/dot_general | solution.py:329
  158.6 0.0 copy-done.4
  158.6 11.3 %fusion.12 = f32[1,4,2,192,1024]{4,3,2,1,0:T(8,128)} fusion(f32[4,2,192,768]{3,2,1,0:T(8,128)} %bitcast.54, f32[1024,768]{0,1:T(8,128)S(1)} %copy-done.4), kind=kOutput, calls=%fused_computation.14 | convolution fusion | flops 7247757312 | bytes 14155776 | tf_op jit(solution)/shard_map/dot_general | solution.py:329
  169.9 0.0 slice-start.2
  169.9 6.2 %copy.13 = f32[1536,768]{1,0:T(8,128)} copy(f32[1536,768]{0,1:T(8,128)} %bitcast.45) | data formatting | bytes 9437184 | tf_op jit(solution)/shard_map/dot_general | solution.py:329
  176.1 0.0 slice-start.3
  176.1 12.2 %fusion.9 = f32[1,4,2,192,1024]{4,3,2,1,0:T(8,128)} fusion(f32[4,2,192,768]{3,2,1,0:T(8,128)} %bitcast.53, f32[1024,768]{0,1:T(8,128)} %copy-done.3), kind=kOutput, calls=%fused_computation.13 | convolution fusion | flops 7247757312 | bytes 14155776 | tf_op jit(solution)/shard_map/dot_general | solution.py:329
  188.3 0.0 slice-done.2
  188.3 0.0 slice-done.3
  188.3 9.4 %pad_maximum_fusion.dx = f32[2,4,2,192,1024]{4,3,2,1,0:T(8,128)} fusion(f32[1,4,2,192,1024]{4,3,2,1,0:T(8,128)S(1)} %bitcast.52, f32[1,4,2,192,1024]{4,3,2,1,0:T(8,128)} %fusion.9), kind=kLoop, calls=%fused_computation | loop fusion | flops 3145728 | bytes 25165824 | tf_op jit(solution)/shard_map/stack | solution.py:347
  197.7 131.2 %shard_map.51 = (f32[192,1536]{1,0:T(8,128)}, f32[192,1024]{1,0:T(8,128)}) custom-call(f32[4,2,192,1536]{3,2,1,0:T(8,128)} %pad_maximum_fusion.1.dw, f32[2,4,2,192,1024]{4,3,2,1,0:T(8,128)} %pad_maximum_fusion.dx), custom_call_target="tpu_custom_call" | custom-call | tf_op jit(solution)/shard_map/pallas_call | solution.py:306
  328.8 2.1 copy.24
  330.9 2.4 copy.25
  (2 shorter events, 0.0 us)
Async XLA Ops:
  102.1 18.9 %slice-start = ((s8[6291456]{0:T(1024)(128)(4,1)}), s8[4194304]{0:T(1024)(128)(4,1)S(1)}, s32[]{:S(2)}) async-start(s8[6291456]{0:T(1024)(128)(4,1)} %bitcast.49), calls=%async_computation | async-start | bytes 8388608
  106.9 14.1 %copy-start = (f32[4,1,192,1536]{3,2,1,0:T(8,128)}, f32[4,1,192,1536]{3,2,1,0:T(8,128)S(1)}, u32[]{:S(2)}) copy-start(f32[4,1,192,1536]{3,2,1,0:T(8,128)S(1)} %get-tuple-element.10) | copy-start | bytes 14155780
  106.9 14.1 %copy-start.1 = (f32[4,1,192,1536]{3,2,1,0:T(8,128)}, f32[4,1,192,1536]{3,2,1,0:T(8,128)S(1)}, u32[]{:S(2)}) copy-start(f32[4,1,192,1536]{3,2,1,0:T(8,128)S(1)} %get-tuple-element.11) | copy-start | bytes 14155780
  106.9 14.1 %slice-start.1 = ((s8[6291456]{0:T(1024)(128)(4,1)}), s8[2097152]{0:T(1024)(128)(4,1)S(1)}, s32[]{:S(2)}) async-start(s8[6291456]{0:T(1024)(128)(4,1)} %bitcast.49), calls=%async_computation.1 | async-start | bytes 4194304
  121.0 10.8 %copy-start.2 = (f32[1024,1536]{1,0:T(8,128)S(1)}, f32[1024,1536]{1,0:T(8,128)}, u32[]{:S(2)}) copy-start(f32[1024,1536]{1,0:T(8,128)} %get-tuple-element.7) | copy-start | bytes 18874372
  131.8 8.2 %copy-start.3 = (f32[1024,768]{0,1:T(8,128)}, f32[1024,768]{0,1:T(8,128)S(1)}, u32[]{:S(2)}) copy-start(f32[1024,768]{0,1:T(8,128)S(1)} %fusion.4) | copy-start | bytes 9437188
  152.4 6.2 %copy-start.4 = (f32[1024,768]{0,1:T(8,128)S(1)}, f32[1024,768]{0,1:T(8,128)}, u32[]{:S(2)}) copy-start(f32[1024,768]{0,1:T(8,128)} %copy-done.3) | copy-start | bytes 9437188
  169.9 18.4 %slice-start.2 = ((s8[6291456]{0:T(1024)(128)(4,1)}), s8[2097152]{0:T(1024)(128)(4,1)S(1)}, s32[]{:S(2)}) async-start(s8[6291456]{0:T(1024)(128)(4,1)} %bitcast.51), calls=%async_computation.2 | async-start | bytes 4194304
  176.1 12.2 %slice-start.3 = ((s8[6291456]{0:T(1024)(128)(4,1)}), s8[4194304]{0:T(1024)(128)(4,1)S(1)}, s32[]{:S(2)}) async-start(s8[6291456]{0:T(1024)(128)(4,1)} %bitcast.51), calls=%async_computation.3 | async-start | bytes 8388608

commit v2 on v0

v2 whole, which is shorter than its diff:
```python
import jax
import jax.numpy as jnp
from jax import lax
from jax.experimental import pallas as pl
from jax.experimental.pallas import tpu as pltpu
from jax.sharding import Mesh
from jax.sharding import PartitionSpec as P

AXES = ("x", "zl", "zh", "y", "c")
MESH = pl.DeviceIdType.MESH
PIECES = 3

inv_sqrt_two = 0.7071067811865476
inv_sqrt_two_pi = 0.3989422804014327


class Place:
    def __init__(self):
        self.x, self.zl, self.zh, self.y, self.c = (lax.axis_index(a) for a in AXES)
        self.z = 2 * self.zh + self.zl
        self.inner = self.zl != self.zh
        self.outer = self.zl == self.zh
        self.to_inner = self.at_z(self.z + 1 - 2 * self.zh)
        self.to_outer = self.at_z(3 * self.zh)
        self.x_plus = [lax.rem(self.x + d, 4) for d in range(4)]
        self.y_plus = [lax.rem(self.y + d, 4) for d in range(4)]
        self.known = {}
        for key in ((1, 0, 0, 0), (-1, 0, 0, 0), (0, 1, 0, 0), (0, -1, 0, 0), (0, 0, 1, 0), (0, 0, -1, 0), (0, 0, 2, 0), (0, 0, 0, 1)):
            self.known[key] = self.place(*key)

    def at_z(self, z):
        return (self.x, lax.rem(z, 2), lax.div(z, 2), self.y, self.c)

    def step(self, dx=0, dy=0, dz=0, dc=0):
        return self.known[dx, dy, dz, dc]

    def place(self, dx, dy, dz, dc):
        z = lax.rem(self.z + dz + 4, 4)
        return (
            lax.rem(self.x + dx + 4, 4),
            lax.rem(z, 2),
            lax.div(z, 2),
            lax.rem(self.y + dy + 4, 4),
            lax.rem(self.c + dc, 2),
        )


def enter(me):
    barrier = pltpu.get_barrier_semaphore()
    steps = [
        dict(dx=1), dict(dx=-1), dict(dy=1), dict(dy=-1),
        dict(dz=1), dict(dz=-1), dict(dz=2), dict(dc=1),
    ]
    for step in steps:
        pl.semaphore_signal(barrier, inc=1, device_id=me.step(**step), device_id_type=MESH)
    pl.semaphore_wait(barrier, len(steps))


def remote(src, dst, send, recv, device):
    return pltpu.make_async_remote_copy(
        src_ref=src, dst_ref=dst, send_sem=send, recv_sem=recv, device_id=device, device_id_type=MESH
    )


def dot(left, right, left_dim, right_dim):
    return lax.dot_general(
        left, right, (((left_dim,), (right_dim,)), ((), ())), preferred_element_type=jnp.float32
    )


def gelu_slope(preact):
    cumulative = 0.5 * (1.0 + lax.erf(preact * inv_sqrt_two))
    density = jnp.exp(-0.5 * preact * preact) * inv_sqrt_two_pi
    return cumulative + preact * density


def split(value):
    high = value.astype(jnp.bfloat16)
    return high, (value - high.astype(jnp.float32)).astype(jnp.bfloat16)


def strips(count, size, body):
    def one(i, carry):
        body(pl.multiple_of(i * size, size))
        return carry

    lax.fori_loop(0, count, one, 0)


def kernel(
    inputs, wt, cot, wout, xout, xo, wf,
    wh, wl, gh, gl, dw, far, near, zin, cin, yfar, ynear, xz,
    zs, zr, fs, xs, xr, gs, gr, s1, r1, sy, ry, sf, rf, sc, rc, ls,
    pfs, pfr, pns, pnr, qs, qr, os_, cs, cr, yfs, yfr, yns, ynr, s2, r2,
):
    me = Place()
    r, half = wt.shape
    tokens = inputs.shape[0]
    rows = r // PIECES
    cols = half // PIECES
    tok = tokens // 8
    dirs = ((0, 1), (1, -1))

    def piece(p):
        return pl.ds(p * rows, rows)

    def block(p):
        return pl.ds(p * cols, cols)

    def part(y, c):
        return pl.ds((y * 2 + c) * tok, tok)

    def y_at(d):
        return me.y_plus[d % 4]

    enter(me)

    slot = me.zl + me.zh - 2 * me.zl * me.zh
    for p in range(PIECES):
        remote(wt.at[piece(p)], wf.at[0, slot, piece(p)], zs.at[p], zr.at[slot, p], me.to_inner).start()

        @pl.when(me.outer)
        def _():
            pltpu.make_async_copy(wt.at[piece(p)], wf.at[0, 0, piece(p)], zr.at[0, p]).start()

    mine = part(me.y, me.c)
    first = remote(inputs.at[mine], xo.at[mine], s1, r1, me.step(dz=2))
    first.start()

    def spread(k):
        s = slot * (k % 2) + (1 - slot) * (k // PIECES)
        p = slot * (k // 2) + (1 - slot) * (k % PIECES)
        here = wf.at[0, s, piece(p)]
        pltpu.make_async_copy(here, here, zr.at[s, p]).wait()

        @pl.when(me.inner & (s == 1))
        def _():
            remote(here, here, fs.at[p], zr.at[s, p], me.to_outer).start()

        for d, dx in dirs:
            remote(here, wf.at[1 + d, s, piece(p)], xs.at[d, s, p], xr.at[d, s, p], me.step(dx=dx)).start()

    def pass_on(p):
        for d, dx in dirs:
            there = wf.at[1 + d, d, piece(p)]
            remote(there, there, gs.at[d, p], xr.at[d, d, p], me.step(dx=dx)).wait_recv()
            remote(there, wf.at[3, d, piece(p)], gs.at[d, p], gr.at[d, p], me.step(dx=dx)).start()

    def straight(d, p):
        return remote(
            dw.at[2 - d, 1 - d, :, block(p)], near.at[d, 1 - d, :, block(p)],
            pns.at[d, 1 - d, p], pnr.at[d, 1 - d, p], me.step(dx=dirs[d][1]),
        )

    def opposite(d, p):
        return remote(
            dw.at[3, d, :, block(p)], far.at[d, :, block(p)], pfs.at[d, p], pfr.at[d, p], me.step(dx=dirs[d][1])
        )

    def onward(d, p):
        return remote(
            far.at[d, :, block(p)], near.at[d, d, :, block(p)], pns.at[d, d, p], pnr.at[d, d, p], me.step(dx=dirs[d][1])
        )

    def compute(xh, xl, stage, cstage):
        def split_inputs(source, s):
            n = 128
            loads = [
                pltpu.make_async_copy(source.at[pl.ds(i * n, n)], stage.at[i % 2, pl.ds(0, n)], ls.at[i % 2])
                for i in range(tokens // n)
            ]
            loads[0].start()
            for i in range(tokens // n):
                if i + 1 < len(loads):
                    loads[i + 1].start()
                loads[i].wait()

                def strip(at):
                    high, low = split(stage[i % 2, pl.ds(at, 16)])
                    to = pl.ds(pl.multiple_of(i * n + at, 16), 16)
                    xh[to, s * half : (s + 1) * half] = high
                    xl[to, s * half : (s + 1) * half] = low

                strips(n // 16, 16, strip)

        def split_weight(units):
            loads = [
                pltpu.make_async_copy(wf.at[j, s], stage.at[i % 2], ls.at[i % 2]) for i, (j, s) in enumerate(units)
            ]
            loads[0].start()
            for i, (j, s) in enumerate(units):
                if i + 1 < len(loads):
                    loads[i + 1].start()
                loads[i].wait()

                def strip(at):
                    high, low = split(stage[i % 2, pl.ds(at, 16)])
                    to = pl.ds(pl.multiple_of(j * r + at, 16), 16)
                    wh[to, s * half : (s + 1) * half] = high
                    wl[to, s * half : (s + 1) * half] = low

                strips(r // 16, 16, strip)

        def turn_cotangent(j):
            column = me.x_plus[(0, 3, 1, 2)[j]] * (2 * r)
            n = cstage.shape[1]
            loads = [
                pltpu.make_async_copy(
                    cot.at[pl.ds(i * n, n), pl.ds(pl.multiple_of(column, 128), 2 * r)], cstage.at[i % 2], ls.at[i % 2]
                )
                for i in range(tokens // n)
            ]
            loads[0].start()
            for i in range(len(loads)):
                if i + 1 < len(loads):
                    loads[i + 1].start()
                loads[i].wait()
                turned = cstage[i % 2].T
                dw[j, 1, :, i * n : (i + 1) * n] = jnp.where(me.zh == 0, turned[:r], turned[r:])

        def preact(j, count, s):
            of = slice(s * half, (s + 1) * half)

            def tile(at):
                to = pl.ds(at, 256)
                left = slice(j * r, (j + count) * r)
                value = (
                    dot(wh[left, of], xh[to, of], 1, 1)
                    + dot(wl[left, of], xh[to, of], 1, 1)
                    + dot(wh[left, of], xl[to, of], 1, 1)
                )
                for i in range(count):
                    new = value[i * r : (i + 1) * r]
                    dw[j + i, 0, :, to] = new if s == 0 else dw[j + i, 0, :, to] + new

            strips(tokens // 256, 256, tile)

        def pre_grad(j):
            def strip(at):
                from_ = pl.ds(at, 16)
                grad = dw[j, 1, from_, :tokens] * gelu_slope(dw[j, 0, from_, :tokens])
                to = pl.ds(pl.multiple_of(j * r + at, 16), 16)
                gh[to], gl[to] = split(grad)

            strips(r // 16, 16, strip)

        def weight_grad(j, count, s, p):
            left = slice(j * r, (j + count) * r)

            def tile(at):
                of = pl.ds(pl.multiple_of(s * half + p * cols + at, 256), 256)
                value = (
                    dot(gh[left], xh[:, of], 1, 0) + dot(gl[left], xh[:, of], 1, 0) + dot(gh[left], xl[:, of], 1, 0)
                )
                to = pl.ds(pl.multiple_of(p * cols + at, 256), 256)
                for i in range(count):
                    dw[j + i, s, :, to] = value[i * r : (i + 1) * r]

            strips(cols // 256, 256, tile)

        spread(0)
        spread(1)
        split_inputs(inputs, 0)
        spread(2)
        spread(3)
        turn_cotangent(0)
        spread(4)
        spread(5)
        first.wait_recv()
        across = [remote(xo.at[mine], xo.at[mine], sy.at[d], ry.at[d], me.step(dy=dy)) for d, dy in dirs]
        for copy in across:
            copy.start()
        shares = [remote(xo.at[mine], xo.at[mine], sc.at[0], rc.at[0], me.step(dc=1))]
        shares[0].start()
        split_weight([(0, 0), (0, 1)])
        preact(0, 1, 0)
        pass_on(0)
        turn_cotangent(1)
        halves = []
        for d, dy in dirs:
            across[d].wait_recv()
            from_y = y_at(-dy)
            rows_of = pl.ds((from_y * 2 + me.c) * tok + d * (tok // 2), tok // 2)
            halves.append(remote(xo.at[rows_of], xo.at[rows_of], sf.at[d], rf.at[d], me.step(dy=dy)))
            halves[-1].start()
            whole = part(from_y, me.c)
            shares.append(remote(xo.at[whole], xo.at[whole], sc.at[1 + d], rc.at[1 + d], me.step(dc=1)))
            shares[-1].start()
        turn_cotangent(2)
        pass_on(1)
        turn_cotangent(3)
        across_far = part(y_at(2), me.c)
        for d in range(2):
            halves[d].wait_recv()
        shares.append(remote(xo.at[across_far], xo.at[across_far], sc.at[3], rc.at[3], me.step(dc=1)))
        shares[-1].start()
        for copy in shares:
            copy.wait_recv()
        split_inputs(xo, 1)
        pass_on(2)
        for d in range(2):
            for p in range(PIECES):
                unit = wf.at[1 + d, 1 - d, piece(p)]
                remote(unit, unit, xs.at[d, 1 - d, p], xr.at[d, 1 - d, p], me.step(dc=1)).wait_recv()
        split_weight([(1, 0), (1, 1), (2, 0), (2, 1)])
        preact(0, 1, 1)
        pre_grad(0)
        preact(1, 2, 0)
        preact(1, 2, 1)
        pre_grad(1)
        pre_grad(2)
        for p in range(PIECES):
            for d, step in dirs:
                weight_grad(2 - d, 1, 1 - d, p)
                straight(d, p).start()
        for d in range(2):
            for p in range(PIECES):
                unit = wf.at[3, d, piece(p)]
                remote(unit, unit, gs.at[d, p], gr.at[d, p], me.step(dc=1)).wait_recv()
        split_weight([(3, 0), (3, 1)])
        preact(3, 1, 0)
        preact(3, 1, 1)
        pre_grad(3)
        for p in range(PIECES):
            for d, step in dirs:
                weight_grad(3, 1, d, p)
                opposite(d, p).start()
        for p in range(PIECES):
            for d, step in dirs:
                weight_grad(2 - d, 1, d, p)
        for p in range(PIECES):
            for s in range(2):
                weight_grad(0, 1, s, p)
        for p in range(PIECES):
            remote(wt.at[piece(p)], wt.at[piece(p)], zs.at[p], zs.at[p], me.step(dc=1)).wait_send()

            @pl.when(me.inner)
            def _():
                remote(wt.at[piece(p)], wt.at[piece(p)], fs.at[p], fs.at[p], me.step(dc=1)).wait_send()

            for d in range(2):
                for s in range(2):
                    remote(wt.at[piece(p)], wt.at[piece(p)], xs.at[d, s, p], xs.at[d, s, p], me.step(dc=1)).wait_send()
                remote(wt.at[piece(p)], wt.at[piece(p)], gs.at[d, p], gs.at[d, p], me.step(dc=1)).wait_send()
        for copy in across + halves + shares + [first]:
            copy.wait_send()

    f32, bf16 = jnp.float32, jnp.bfloat16
    pl.run_scoped(
        compute,
        pltpu.VMEM((tokens, 2 * half), bf16), pltpu.VMEM((tokens, 2 * half), bf16),
        pltpu.VMEM((2, r, half), f32), pltpu.VMEM((2, 256, 2 * r), f32),
    )

    def sums(acc):
        order = [(s, dy) for s in (1, 0) for dy in (2, 1, -1, 0)]
        shares = []
        y_copies = {}
        left = pl.ds(0, tokens // 2)
        right = pl.ds(tokens // 2, tokens // 2)
        side = (left, right)
        own = pl.ds(pl.multiple_of(me.c * r, r), r)
        others = pl.ds(pl.multiple_of((1 - me.c) * r, r), r)

        def input_grad(i):
            s, dy = order[i]
            of = pl.ds(pl.multiple_of(s * half + y_at(dy) * (2 * r), 128), 2 * r)
            acc[i] = dot(wh[:, of], gh[...], 0, 0) + dot(wl[:, of], gh[...], 0, 0) + dot(wh[:, of], gl[...], 0, 0)
            copy = remote(acc.at[i, others], cin.at[i], cs.at[i], cr.at[i], me.step(dc=1))
            copy.start()
            shares.append(copy)

        def on_chip(i):
            shares[i].wait_recv()
            acc[i, own] = acc[i, own] + cin[i]

        def y_start(i, d, kind, source, target, sems):
            copy = remote(source, target, sems[0], sems[1], me.step(dy=dirs[d][1]))
            copy.start()
            y_copies[i, d, kind] = copy

        def y_far(s):
            i = 4 * (1 - s)
            on_chip(i)
            for d in range(2):
                y_start(s, d, 0, acc.at[i, own, side[d]], yfar.at[s, d], (yfs.at[s, d], yfr.at[s, d]))

        def y_straight(s, d):
            i = 4 * (1 - s) + 1 + d
            on_chip(i)
            o = 1 - d
            y_start(s, d, 1, acc.at[i, own, side[o]], ynear.at[s, d, :, side[o]], (yns.at[s, d, o], ynr.at[s, d, o]))

        def y_pass(s):
            for d in range(2):
                i = 4 * (1 - s) + 1 + d
                y_copies[s, d, 0].wait_recv()
                yfar[s, d] = yfar[s, d] + acc[i, own, side[d]]
                y_start(s, d, 2, yfar.at[s, d], ynear.at[s, d, :, side[d]], (yns.at[s, d, d], ynr.at[s, d, d]))

        def y_sum(s):
            i = 4 * (1 - s) + 3
            for d in range(2):
                y_copies[s, d, 1].wait_recv()
                y_copies[s, d, 2].wait_recv()
            acc[i, own] = acc[i, own] + ynear[s, 0] + ynear[s, 1]

        def x_pass(p):
            for d, step in dirs:
                opposite(d, p).wait_recv()
                far[d, :, block(p)] = far[d, :, block(p)] + dw[2 - d, d, :, block(p)]
                onward(d, p).start()

        input_grad(0)
        input_grad(1)
        y_far(1)
        input_grad(2)
        y_straight(1, 0)
        input_grad(3)
        y_straight(1, 1)
        input_grad(4)
        on_chip(3)
        input_grad(5)
        y_far(0)
        input_grad(6)
        y_straight(0, 0)
        input_grad(7)
        y_straight(0, 1)
        on_chip(7)
        y_pass(1)
        x_pass(0)
        x_pass(1)
        y_pass(0)
        x_pass(2)
        y_sum(1)
        last = remote(acc.at[3, own], xz, s2, r2, me.step(dz=2))
        last.start()

        for p in range(PIECES):
            for d in range(2):
                straight(d, p).wait_recv()
                onward(d, p).wait_recv()
            for s in range(2):
                dw[0, s, :, block(p)] = dw[0, s, :, block(p)] + near[0, s, :, block(p)] + near[1, s, :, block(p)]

            @pl.when(me.outer)
            def _():
                remote(dw.at[0, 1, :, block(p)], zin.at[0, :, block(p)], qs.at[p], qr.at[0, p], me.to_inner).start()

            @pl.when(me.inner)
            def _():
                remote(dw.at[0, 0, :, block(p)], zin.at[1, :, block(p)], qs.at[p], qr.at[1, p], me.to_outer).start()

        y_sum(0)
        for p in range(PIECES):
            @pl.when(me.inner)
            def _():
                here = zin.at[0, :, block(p)]
                remote(here, here, os_.at[p], qr.at[0, p], me.to_inner).wait_recv()
                zin[0, :, block(p)] = dw[0, 1, :, block(p)] + zin[0, :, block(p)]
                remote(here, zin.at[1, :, block(p)], os_.at[p], qr.at[1, p], me.to_inner).start()

        last.wait_recv()
        acc[7, own] = acc[7, own] + xz[...]
        x_out = pltpu.make_async_copy(acc.at[7, own], xout, ls.at[0])
        x_out.start()
        for p in range(PIECES):
            here = zin.at[1, :, block(p)]
            remote(here, here, qs.at[p], qr.at[1, p], me.step(dz=1)).wait_recv()

            @pl.when(me.outer)
            def _():
                zin[1, :, block(p)] = dw[0, 0, :, block(p)] + zin[1, :, block(p)]

        w_out = pltpu.make_async_copy(zin.at[1], wout, ls.at[1])
        w_out.start()

        for p in range(PIECES):
            here = zin.at[1, :, block(p)]
            remote(here, here, qs.at[p], qr.at[1, p], me.step(dz=1)).wait_send()

            @pl.when(me.inner)
            def _():
                remote(here, here, os_.at[p], qr.at[0, p], me.step(dz=1)).wait_send()

        for p in range(PIECES):
            for d in range(2):
                for copy in (opposite(d, p), straight(d, p), onward(d, p)):
                    copy.wait_send()
        for copy in list(y_copies.values()) + shares + [last]:
            copy.wait_send()
        x_out.wait()
        w_out.wait()

    pl.run_scoped(sums, pltpu.VMEM((8, 2 * r, tokens), f32))


def fused(inputs, wt, cot):
    dma = pltpu.SemaphoreType.DMA
    vmem = pltpu.VMEM
    f32, bf16 = jnp.float32, jnp.bfloat16
    r, d = wt.shape
    t = inputs.shape[0]
    hbm = pl.BlockSpec(memory_space=pltpu.HBM)
    n = PIECES
    return pl.pallas_call(
        kernel,
        out_shape=(
            jax.ShapeDtypeStruct((r, d), f32),
            jax.ShapeDtypeStruct((r, t), f32),
            jax.ShapeDtypeStruct((t, d), f32),
            jax.ShapeDtypeStruct((4, 2, r, d), f32),
        ),
        in_specs=[hbm] * 3,
        out_specs=(hbm,) * 4,
        scratch_shapes=[
            vmem((4 * r, 2 * d), bf16), vmem((4 * r, 2 * d), bf16), vmem((4 * r, t), bf16), vmem((4 * r, t), bf16),
            vmem((4, 2, r, d), f32), vmem((2, r, d), f32), vmem((2, 2, r, d), f32), vmem((2, r, d), f32),
            vmem((8, r, t), f32), vmem((2, 2, r, t // 2), f32), vmem((2, 2, r, t), f32), vmem((r, t), f32),
            dma((n,)), dma((2, n)), dma((n,)), dma((2, 2, n)), dma((2, 2, n)), dma((2, n)), dma((2, n)),
            dma, dma, dma((2,)), dma((2,)), dma((2,)), dma((2,)), dma((4,)), dma((4,)), dma((2,)),
            dma((2, n)), dma((2, n)), dma((2, 2, n)), dma((2, 2, n)), dma((n,)), dma((2, n)), dma((n,)),
            dma((8,)), dma((8,)), dma((2, 2)), dma((2, 2)), dma((2, 2, 2)), dma((2, 2, 2)), dma, dma,
        ],
        compiler_params=pltpu.CompilerParams(collective_id=0, has_side_effects=True, vmem_limit_bytes=60 << 20),
    )(inputs, wt, cot)[:2]


def local(inputs, weight, cotangent):
    wout, xout = fused(inputs, weight.T, cotangent)
    return (xout.T, wout.T)


def solution(mesh):
    torus = Mesh(mesh.devices.reshape(4, 2, 2, 4, 2), AXES)
    in_specs = (P(("x", "zl"), "zh"), P("zh", ("y", "c", "x", "zl")), P(("x", "zl"), ("y", "c")))
    out_specs = (P(("x", "zl"), ("zh", "y", "c")), P("zh", ("y", "c", "x", "zl")))
    return jax.shard_map(local, mesh=torus, in_specs=in_specs, out_specs=out_specs, check_vma=False)
```

time: 628 us -> 246 us (0.39)
  waiting for transfers between devices: 489 us -> 0 us
  Pallas kernels: 0 us -> 241 us
  matrix products: 105 us -> 0 us
  between operations: 13.8 us -> 0.64 us
  other arithmetic: 7.38 us -> 0 us
  starting transfers between devices: 6.88 us -> 0 us
    all_gather x2 -> x0, waiting for transfers between devices: 279 us -> none  [the longest x1 191 us: local(): full_weight = lax.all_gather(weight, DEPTH, axis=1, tiled=True)]
    pallas_call x0 -> x1, Pallas kernels: none -> 241 us  [fused(): pl.pallas_call(kernel, out_shape=(jax.ShapeDtypeStruct((r, d), f32), jax....]
    reduce_scatter x3 -> x0, waiting for transfers between devices: 138 us -> none  [the longest x2 92.6 us: sum_by_axis(): so_far = lax.psum_scatter(so_far, axis, scatter_dimension=0, tiled=True)]
    dot_general x3 -> x0, matrix products: 105 us -> none  [the longest x1 35.7 us: product_first(): lax.dot_general(left, right, (((0,), (0,)), ((), ())), precision=lax.Prec...]
    all_to_all x1 -> x0, waiting for transfers between devices: 71.3 us -> none  [sum_at_owner(): tiles = lax.all_to_all(cut_along(shard, dim, count), axis, 0, 0, tiled=True)]
  transfers between devices with their start and end apart: 6 -> 0, of which waited for: 6 -> 0; matrix products, arithmetic and copies ran while one was open for 6% -> 0% of each run, Pallas kernels for 0% -> 0%
where the time goes in v2:
time: 246 us
  Pallas kernels  241 us (98%)
  local copies, waits for them, and re-layouts  4.45 us (2%)
    pallas_call x1, Pallas kernels, fused(): pl.pallas_call(kernel, out_shape=(jax.ShapeDtypeStruct((r, d), f32), jax....  241 us

profile of v2, /device:TPU:32, one launch (start us, length us, event | category | flops | bytes accessed | tf_op | source)
XLA Modules:
  0.0 245.7 jit_solution(12950309894887471941)
XLA Ops:
  0.6 240.6 %shard_map.50 = (f32[192,1536]{1,0:T(8,128)}, f32[192,1024]{1,0:T(8,128)}, f32[1024,1536]{1,0:T(8,128)}, f32[4,2,192,1536]{3,2,1,0:T(8,128)}) custom-call(f32[1024,1536]{1,0:T(8,128)} %inputs.1, f32[192,1536]{1,0:T(8,128)} %bitcast.4, f32[1024,1536]{1,0:T(8,128)} %cot.1), custom_call_target="tpu_custom_call" | custom-call | tf_op jit(solution)/shard_map/pallas_call | solution.py:506
  241.2 2.1 copy.7
  243.3 2.4 copy.8

commit v3 on v2

--- a/solution.py
+++ b/solution.py
@@ -8,7 +8,7 @@
 
 AXES = ("x", "zl", "zh", "y", "c")
 MESH = pl.DeviceIdType.MESH
-PIECES = 3
+PIECES = 6
 
 inv_sqrt_two = 0.7071067811865476
 inv_sqrt_two_pi = 0.3989422804014327
@@ -107,25 +107,45 @@
     def block(p):
         return pl.ds(p * cols, cols)
 
-    def part(y, c):
-        return pl.ds((y * 2 + c) * tok, tok)
-
     def y_at(d):
         return me.y_plus[d % 4]
 
     enter(me)
 
     slot = me.zl + me.zh - 2 * me.zl * me.zh
-    for p in range(PIECES):
+    def send_unit(p):
         remote(wt.at[piece(p)], wf.at[0, slot, piece(p)], zs.at[p], zr.at[slot, p], me.to_inner).start()
 
         @pl.when(me.outer)
         def _():
             pltpu.make_async_copy(wt.at[piece(p)], wf.at[0, 0, piece(p)], zr.at[0, p]).start()
 
-    mine = part(me.y, me.c)
-    first = remote(inputs.at[mine], xo.at[mine], s1, r1, me.step(dz=2))
-    first.start()
+    step_rows = tok // 2
+
+    def rows_of(y, h):
+        return pl.ds((y * 2 + me.c) * tok + h * step_rows, step_rows)
+
+    def fetch(h):
+        at = rows_of(me.y, h)
+        return remote(inputs.at[at], xo.at[at], s1.at[h], r1.at[h], me.step(dz=2))
+
+    def across(h, d):
+        at = rows_of(me.y, h)
+        return remote(xo.at[at], xo.at[at], sy.at[h, d], ry.at[h, d], me.step(dy=dirs[d][1]))
+
+    def onto(h, d):
+        at = pl.ds((y_at(-dirs[d][1]) * 2 + me.c) * tok + h * step_rows + d * (step_rows // 2), step_rows // 2)
+        return remote(xo.at[at], xo.at[at], sf.at[h, d], rf.at[h, d], me.step(dy=dirs[d][1]))
+
+    def share(h, k):
+        at = rows_of(y_at((0, -1, 1, 2)[k]), h)
+        return remote(xo.at[at], xo.at[at], sc.at[h, k], rc.at[h, k], me.step(dc=1))
+
+    for h in range(2):
+        send_unit(3 * h)
+        send_unit(3 * h + 1)
+        fetch(h).start()
+        send_unit(3 * h + 2)
 
     def spread(k):
         s = slot * (k % 2) + (1 - slot) * (k // PIECES)
@@ -244,75 +264,87 @@
 
             strips(r // 16, 16, strip)
 
-        def weight_grad(j, count, s, p):
+        def weight_grad(j, count, s, first, tiles):
             left = slice(j * r, (j + count) * r)
+            wide = 2 * cols
 
             def tile(at):
-                of = pl.ds(pl.multiple_of(s * half + p * cols + at, 256), 256)
+                to = pl.ds(pl.multiple_of(first * wide + at, wide), wide)
+                of = pl.ds(pl.multiple_of(s * half + first * wide + at, wide), wide)
                 value = (
                     dot(gh[left], xh[:, of], 1, 0) + dot(gl[left], xh[:, of], 1, 0) + dot(gh[left], xl[:, of], 1, 0)
                 )
-                to = pl.ds(pl.multiple_of(p * cols + at, 256), 256)
                 for i in range(count):
                     dw[j + i, s, :, to] = value[i * r : (i + 1) * r]
 
-            strips(cols // 256, 256, tile)
-
-        spread(0)
-        spread(1)
+            strips(tiles, wide, tile)
+
+        def fetched(h):
+            fetch(h).wait_recv()
+            for d in range(2):
+                across(h, d).start()
+            share(h, 0).start()
+
+        def crossed(h):
+            for d in range(2):
+                across(h, d).wait_recv()
+                onto(h, d).start()
+                share(h, 1 + d).start()
+
+        def met(h):
+            for d in range(2):
+                onto(h, d).wait_recv()
+            share(h, 3).start()
+
+        for k in range(4):
+            spread(k)
         split_inputs(inputs, 0)
-        spread(2)
-        spread(3)
+        fetched(0)
+        for k in range(4, 8):
+            spread(k)
         turn_cotangent(0)
-        spread(4)
-        spread(5)
-        first.wait_recv()
-        across = [remote(xo.at[mine], xo.at[mine], sy.at[d], ry.at[d], me.step(dy=dy)) for d, dy in dirs]
-        for copy in across:
-            copy.start()
-        shares = [remote(xo.at[mine], xo.at[mine], sc.at[0], rc.at[0], me.step(dc=1))]
-        shares[0].start()
+        turn_cotangent(1)
+        crossed(0)
+        fetched(1)
+        turn_cotangent(2)
+        met(0)
+        for k in range(8, 12):
+            spread(k)
+        turn_cotangent(3)
+        pass_on(0)
         split_weight([(0, 0), (0, 1)])
+        crossed(1)
         preact(0, 1, 0)
-        pass_on(0)
-        turn_cotangent(1)
-        halves = []
-        for d, dy in dirs:
-            across[d].wait_recv()
-            from_y = y_at(-dy)
-            rows_of = pl.ds((from_y * 2 + me.c) * tok + d * (tok // 2), tok // 2)
-            halves.append(remote(xo.at[rows_of], xo.at[rows_of], sf.at[d], rf.at[d], me.step(dy=dy)))
-            halves[-1].start()
-            whole = part(from_y, me.c)
-            shares.append(remote(xo.at[whole], xo.at[whole], sc.at[1 + d], rc.at[1 + d], me.step(dc=1)))
-            shares[-1].start()
-        turn_cotangent(2)
         pass_on(1)
-        turn_cotangent(3)
-        across_far = part(y_at(2), me.c)
-        for d in range(2):
-            halves[d].wait_recv()
-        shares.append(remote(xo.at[across_far], xo.at[across_far], sc.at[3], rc.at[3], me.step(dc=1)))
-        shares[-1].start()
-        for copy in shares:
-            copy.wait_recv()
+        met(1)
+        pass_on(2)
+        for h in range(2):
+            for k in range(4):
+                share(h, k).wait_recv()
         split_inputs(xo, 1)
-        pass_on(2)
+        preact(0, 1, 1)
+        pre_grad(0)
+        pass_on(3)
+        weight_grad(0, 1, 0, 0, 3)
+        pass_on(4)
+        weight_grad(0, 1, 1, 0, 3)
+        pass_on(5)
         for d in range(2):
             for p in range(PIECES):
                 unit = wf.at[1 + d, 1 - d, piece(p)]
                 remote(unit, unit, xs.at[d, 1 - d, p], xr.at[d, 1 - d, p], me.step(dc=1)).wait_recv()
         split_weight([(1, 0), (1, 1), (2, 0), (2, 1)])
-        preact(0, 1, 1)
-        pre_grad(0)
         preact(1, 2, 0)
         preact(1, 2, 1)
         pre_grad(1)
         pre_grad(2)
-        for p in range(PIECES):
-            for d, step in dirs:
-                weight_grad(2 - d, 1, 1 - d, p)
-                straight(d, p).start()
+        for p in range(PIECES // 2):
+            for d in range(2):
+                weight_grad(2 - d, 1, 1 - d, p, 1)
+                straight(d, 2 * p).start()
+                straight(d, 2 * p + 1).start()
+        for d in range(2):
+            weight_grad(2 - d, 1, d, 0, 3)
         for d in range(2):
             for p in range(PIECES):
                 unit = wf.at[3, d, piece(p)]
@@ -321,29 +353,11 @@
         preact(3, 1, 0)
         preact(3, 1, 1)
         pre_grad(3)
-        for p in range(PIECES):
-            for d, step in dirs:
-                weight_grad(3, 1, d, p)
-                opposite(d, p).start()
-        for p in range(PIECES):
-            for d, step in dirs:
-                weight_grad(2 - d, 1, d, p)
-        for p in range(PIECES):
-            for s in range(2):
-                weight_grad(0, 1, s, p)
-        for p in range(PIECES):
-            remote(wt.at[piece(p)], wt.at[piece(p)], zs.at[p], zs.at[p], me.step(dc=1)).wait_send()
-
-            @pl.when(me.inner)
-            def _():
-                remote(wt.at[piece(p)], wt.at[piece(p)], fs.at[p], fs.at[p], me.step(dc=1)).wait_send()
-
-            for d in range(2):
-                for s in range(2):
-                    remote(wt.at[piece(p)], wt.at[piece(p)], xs.at[d, s, p], xs.at[d, s, p], me.step(dc=1)).wait_send()
-                remote(wt.at[piece(p)], wt.at[piece(p)], gs.at[d, p], gs.at[d, p], me.step(dc=1)).wait_send()
-        for copy in across + halves + shares + [first]:
-            copy.wait_send()
+        for p in range(PIECES // 2):
+            for d in range(2):
+                weight_grad(3, 1, d, p, 1)
+                opposite(d, 2 * p).start()
+                opposite(d, 2 * p + 1).start()
 
     f32, bf16 = jnp.float32, jnp.bfloat16
     pl.run_scoped(
@@ -427,16 +441,17 @@
         input_grad(7)
         y_straight(0, 1)
         on_chip(7)
-        y_pass(1)
         x_pass(0)
         x_pass(1)
+        y_pass(1)
+        x_pass(2)
+        x_pass(3)
         y_pass(0)
-        x_pass(2)
-        y_sum(1)
+        x_pass(4)
+        x_pass(5)
         last = remote(acc.at[3, own], xz, s2, r2, me.step(dz=2))
-        last.start()
-
-        for p in range(PIECES):
+
+        def x_sum(p):
             for d in range(2):
                 straight(d, p).wait_recv()
                 onward(d, p).wait_recv()
@@ -451,8 +466,7 @@
             def _():
                 remote(dw.at[0, 0, :, block(p)], zin.at[1, :, block(p)], qs.at[p], qr.at[1, p], me.to_outer).start()
 
-        y_sum(0)
-        for p in range(PIECES):
+        def z_pass(p):
             @pl.when(me.inner)
             def _():
                 here = zin.at[0, :, block(p)]
@@ -460,6 +474,15 @@
                 zin[0, :, block(p)] = dw[0, 1, :, block(p)] + zin[0, :, block(p)]
                 remote(here, zin.at[1, :, block(p)], os_.at[p], qr.at[1, p], me.to_inner).start()
 
+        for p in range(PIECES):
+            x_sum(p)
+            if p > 0:
+                z_pass(p - 1)
+            if p == 3:
+                y_sum(1)
+                last.start()
+        z_pass(PIECES - 1)
+        y_sum(0)
         last.wait_recv()
         acc[7, own] = acc[7, own] + xz[...]
         x_out = pltpu.make_async_copy(acc.at[7, own], xout, ls.at[0])
@@ -487,6 +510,24 @@
             for d in range(2):
                 for copy in (opposite(d, p), straight(d, p), onward(d, p)):
                     copy.wait_send()
+            unit = wt.at[piece(p)]
+            remote(unit, unit, zs.at[p], zs.at[p], me.step(dc=1)).wait_send()
+
+            @pl.when(me.inner)
+            def _():
+                remote(unit, unit, fs.at[p], fs.at[p], me.step(dc=1)).wait_send()
+
+            for d in range(2):
+                for s in range(2):
+                    remote(unit, unit, xs.at[d, s, p], xs.at[d, s, p], me.step(dc=1)).wait_send()
+                remote(unit, unit, gs.at[d, p], gs.at[d, p], me.step(dc=1)).wait_send()
+        for h in range(2):
+            fetch(h).wait_send()
+            for d in range(2):
+                across(h, d).wait_send()
+                onto(h, d).wait_send()
+            for k in range(4):
+                share(h, k).wait_send()
         for copy in list(y_copies.values()) + shares + [last]:
             copy.wait_send()
         x_out.wait()
@@ -518,7 +559,7 @@
             vmem((4, 2, r, d), f32), vmem((2, r, d), f32), vmem((2, 2, r, d), f32), vmem((2, r, d), f32),
             vmem((8, r, t), f32), vmem((2, 2, r, t // 2), f32), vmem((2, 2, r, t), f32), vmem((r, t), f32),
             dma((n,)), dma((2, n)), dma((n,)), dma((2, 2, n)), dma((2, 2, n)), dma((2, n)), dma((2, n)),
-            dma, dma, dma((2,)), dma((2,)), dma((2,)), dma((2,)), dma((4,)), dma((4,)), dma((2,)),
+            dma((2,)), dma((2,)), dma((2, 2)), dma((2, 2)), dma((2, 2)), dma((2, 2)), dma((2, 4)), dma((2, 4)), dma((2,)),
             dma((2, n)), dma((2, n)), dma((2, 2, n)), dma((2, 2, n)), dma((n,)), dma((2, n)), dma((n,)),
             dma((8,)), dma((8,)), dma((2, 2)), dma((2, 2)), dma((2, 2, 2)), dma((2, 2, 2)), dma, dma,
         ],

time: 246 us -> 215 us (0.87)
  Pallas kernels: 241 us -> 209 us
    pallas_call x1, Pallas kernels: 241 us -> 209 us  [fused(): pl.pallas_call(kernel, out_shape=(jax.ShapeDtypeStruct((r, d), f32), jax....]
where the time goes in v3:
time: 215 us; the launch traced here: 214 us
  Pallas kernels  209 us (97%)
  local copies, waits for them, and re-layouts  4.45 us (2%)
    pallas_call x1, Pallas kernels, fused(): pl.pallas_call(kernel, out_shape=(jax.ShapeDtypeStruct((r, d), f32), jax....  209 us
    unnamed x2, local copies, waits for them, and re-layouts  4.45 us

profile of v3, /device:TPU:32, one launch (start us, length us, event | category | flops | bytes accessed | tf_op | source)
XLA Modules:
  0.0 214.3 jit_solution(16451020265752582966)
XLA Ops:
  0.6 209.2 %shard_map.50 = (f32[192,1536]{1,0:T(8,128)}, f32[192,1024]{1,0:T(8,128)}, f32[1024,1536]{1,0:T(8,128)}, f32[4,2,192,1536]{3,2,1,0:T(8,128)}) custom-call(f32[1024,1536]{1,0:T(8,128)} %inputs.1, f32[192,1536]{1,0:T(8,128)} %bitcast.4, f32[1024,1536]{1,0:T(8,128)} %cot.1), custom_call_target="tpu_custom_call" | custom-call | tf_op jit(solution)/shard_map/pallas_call | solution.py:547
  209.8 2.1 copy.7
  211.9 2.4 %copy.8 = f32[1536,192]{0,1:T(8,128)} copy(f32[1536,192]{0,1:T(8,128)} %bitcast.3) | data formatting | bytes 2359296

commit v4 on v3

--- a/solution.py
+++ b/solution.py
@@ -9,6 +9,7 @@
 AXES = ("x", "zl", "zh", "y", "c")
 MESH = pl.DeviceIdType.MESH
 PIECES = 6
+EARLY = 4
 
 inv_sqrt_two = 0.7071067811865476
 inv_sqrt_two_pi = 0.3989422804014327
@@ -339,12 +340,11 @@
         pre_grad(1)
         pre_grad(2)
         for p in range(PIECES // 2):
-            for d in range(2):
-                weight_grad(2 - d, 1, 1 - d, p, 1)
-                straight(d, 2 * p).start()
-                straight(d, 2 * p + 1).start()
-        for d in range(2):
-            weight_grad(2 - d, 1, d, 0, 3)
+            for d in (1, 0):
+                weight_grad(1, 2, 1 - d, p, 1)
+                if p < EARLY // 2:
+                    straight(d, 2 * p).start()
+                    straight(d, 2 * p + 1).start()
         for d in range(2):
             for p in range(PIECES):
                 unit = wf.at[3, d, piece(p)]
@@ -356,8 +356,9 @@
         for p in range(PIECES // 2):
             for d in range(2):
                 weight_grad(3, 1, d, p, 1)
-                opposite(d, 2 * p).start()
-                opposite(d, 2 * p + 1).start()
+                if p < EARLY // 2:
+                    opposite(d, 2 * p).start()
+                    opposite(d, 2 * p + 1).start()
 
     f32, bf16 = jnp.float32, jnp.bfloat16
     pl.run_scoped(
@@ -428,27 +429,30 @@
         input_grad(0)
         input_grad(1)
         y_far(1)
+        x_pass(0)
+        x_pass(1)
         input_grad(2)
         y_straight(1, 0)
         input_grad(3)
         y_straight(1, 1)
         input_grad(4)
+        x_pass(2)
+        y_pass(1)
         on_chip(3)
         input_grad(5)
         y_far(0)
+        x_pass(3)
+        for p in range(EARLY, PIECES):
+            for d in range(2):
+                opposite(d, p).start()
+        for p in range(EARLY, PIECES):
+            for d in range(2):
+                straight(d, p).start()
         input_grad(6)
         y_straight(0, 0)
         input_grad(7)
         y_straight(0, 1)
         on_chip(7)
-        x_pass(0)
-        x_pass(1)
-        y_pass(1)
-        x_pass(2)
-        x_pass(3)
-        y_pass(0)
-        x_pass(4)
-        x_pass(5)
         last = remote(acc.at[3, own], xz, s2, r2, me.step(dz=2))
 
         def x_sum(p):
@@ -474,14 +478,23 @@
                 zin[0, :, block(p)] = dw[0, 1, :, block(p)] + zin[0, :, block(p)]
                 remote(here, zin.at[1, :, block(p)], os_.at[p], qr.at[1, p], me.to_inner).start()
 
-        for p in range(PIECES):
-            x_sum(p)
-            if p > 0:
-                z_pass(p - 1)
-            if p == 3:
-                y_sum(1)
-                last.start()
-        z_pass(PIECES - 1)
+        x_sum(0)
+        x_sum(1)
+        z_pass(0)
+        x_sum(2)
+        z_pass(1)
+        x_sum(3)
+        z_pass(2)
+        y_sum(1)
+        last.start()
+        z_pass(3)
+        x_pass(4)
+        x_pass(5)
+        y_pass(0)
+        x_sum(4)
+        z_pass(4)
+        x_sum(5)
+        z_pass(5)
         y_sum(0)
         last.wait_recv()
         acc[7, own] = acc[7, own] + xz[...]

time: 215 us -> 205 us (0.953)
  Pallas kernels: 209 us -> 199 us
    pallas_call x1, Pallas kernels: 209 us -> 199 us  [fused(): pl.pallas_call(kernel, out_shape=(jax.ShapeDtypeStruct((r, d), f32), jax....]
where the time goes in v4:
time: 205 us; the launch traced here: 204 us
  Pallas kernels  199 us (97%)
  local copies, waits for them, and re-layouts  4.45 us (2%)
    pallas_call x1, Pallas kernels, fused(): pl.pallas_call(kernel, out_shape=(jax.ShapeDtypeStruct((r, d), f32), jax....  199 us
    unnamed x2, local copies, waits for them, and re-layouts  4.45 us

profile of v4, /device:TPU:32, one launch (start us, length us, event | category | flops | bytes accessed | tf_op | source)
XLA Modules:
  0.0 204.1 jit_solution(8217757049923129230)
XLA Ops:
  0.6 199.1 %shard_map.50 = (f32[192,1536]{1,0:T(8,128)}, f32[192,1024]{1,0:T(8,128)}, f32[1024,1536]{1,0:T(8,128)}, f32[4,2,192,1536]{3,2,1,0:T(8,128)}) custom-call(f32[1024,1536]{1,0:T(8,128)} %inputs.1, f32[192,1536]{1,0:T(8,128)} %bitcast.4, f32[1024,1536]{1,0:T(8,128)} %cot.1), custom_call_target="tpu_custom_call" | custom-call | tf_op jit(solution)/shard_map/pallas_call | solution.py:560
  199.7 2.1 %copy.7 = f32[1024,192]{0,1:T(8,128)} copy(f32[1024,192]{0,1:T(8,128)} %bitcast.5) | data formatting | bytes 1572864
  201.8 2.4 %copy.8 = f32[1536,192]{0,1:T(8,128)} copy(f32[1536,192]{0,1:T(8,128)} %bitcast.3) | data formatting | bytes 2359296

commit v5 on v4

--- a/solution.py
+++ b/solution.py
@@ -9,6 +9,7 @@
 AXES = ("x", "zl", "zh", "y", "c")
 MESH = pl.DeviceIdType.MESH
 PIECES = 6
+UNITS = PIECES - 1
 EARLY = 4
 
 inv_sqrt_two = 0.7071067811865476
@@ -89,10 +90,11 @@
 
 
 def kernel(
-    inputs, wt, cot, wout, xout, xo, wf,
+    inputs, wt, cot, wout, xout, xo, wf, wrow,
     wh, wl, gh, gl, dw, far, near, zin, cin, yfar, ynear, xz,
     zs, zr, fs, xs, xr, gs, gr, s1, r1, sy, ry, sf, rf, sc, rc, ls,
     pfs, pfr, pns, pnr, qs, qr, os_, cs, cr, yfs, yfr, yns, ynr, s2, r2,
+    bxs, bxr, bgs, bgr, bzs, bzr, bfs,
 ):
     me = Place()
     r, half = wt.shape
@@ -142,15 +144,46 @@
         at = rows_of(y_at((0, -1, 1, 2)[k]), h)
         return remote(xo.at[at], xo.at[at], sc.at[h, k], rc.at[h, k], me.step(dc=1))
 
-    for h in range(2):
-        send_unit(3 * h)
-        send_unit(3 * h + 1)
-        fetch(h).start()
-        send_unit(3 * h + 2)
+    turned = piece(UNITS)
+
+    def row_out(d):
+        return remote(wt.at[turned], wrow.at[1 + d], bxs.at[d], bxr.at[d], me.step(dx=dirs[d][1]))
+
+    def row_on(d):
+        at = pl.ds(d * (rows // 2), rows // 2)
+        return remote(wrow.at[1 + d, at], wrow.at[3, at], bgs.at[d], bgr.at[d], me.step(dx=dirs[d][1]))
+
+    def row_z(j):
+        source = wt.at[turned] if j == 0 else wrow.at[j]
+        remote(source, wf.at[j, slot, turned], bzs.at[j], bzr.at[j, slot], me.to_inner).start()
+
+        @pl.when(me.outer)
+        def _():
+            pltpu.make_async_copy(source, wf.at[j, 0, turned], bzr.at[j, 0]).start()
+
+    def row_pass(j):
+        for s in range(2):
+            here = wf.at[j, s, turned]
+            pltpu.make_async_copy(here, here, bzr.at[j, s]).wait()
+
+        @pl.when(me.inner)
+        def _():
+            here = wf.at[j, 1, turned]
+            remote(here, here, bfs.at[j], bzr.at[j, 1], me.to_outer).start()
+
+    for d in range(2):
+        row_out(d).start()
+    send_unit(0)
+    send_unit(1)
+    fetch(0).start()
+    for p in range(2, UNITS):
+        send_unit(p)
+    fetch(1).start()
+    row_z(0)
 
     def spread(k):
-        s = slot * (k % 2) + (1 - slot) * (k // PIECES)
-        p = slot * (k // 2) + (1 - slot) * (k % PIECES)
+        s = slot * (k % 2) + (1 - slot) * (k // UNITS)
+        p = slot * (k // 2) + (1 - slot) * (k % UNITS)
         here = wf.at[0, s, piece(p)]
         pltpu.make_async_copy(here, here, zr.at[s, p]).wait()
 
@@ -299,39 +332,47 @@
 
         for k in range(4):
             spread(k)
+        for d in range(2):
+            row_out(d).wait_recv()
+            row_on(d).start()
+            row_z(1 + d)
         split_inputs(inputs, 0)
         fetched(0)
-        for k in range(4, 8):
+        for k in range(4, 7):
             spread(k)
         turn_cotangent(0)
         turn_cotangent(1)
         crossed(0)
         fetched(1)
+        for d in range(2):
+            row_on(d).wait_recv()
+        row_z(3)
         turn_cotangent(2)
         met(0)
-        for k in range(8, 12):
+        for k in range(7, 2 * UNITS):
             spread(k)
         turn_cotangent(3)
         pass_on(0)
+        row_pass(0)
         split_weight([(0, 0), (0, 1)])
         crossed(1)
         preact(0, 1, 0)
         pass_on(1)
         met(1)
         pass_on(2)
+        row_pass(1)
         for h in range(2):
             for k in range(4):
                 share(h, k).wait_recv()
         split_inputs(xo, 1)
+        pass_on(3)
+        row_pass(2)
         preact(0, 1, 1)
+        pass_on(4)
+        row_pass(3)
         pre_grad(0)
-        pass_on(3)
-        weight_grad(0, 1, 0, 0, 3)
-        pass_on(4)
-        weight_grad(0, 1, 1, 0, 3)
-        pass_on(5)
         for d in range(2):
-            for p in range(PIECES):
+            for p in range(UNITS):
                 unit = wf.at[1 + d, 1 - d, piece(p)]
                 remote(unit, unit, xs.at[d, 1 - d, p], xr.at[d, 1 - d, p], me.step(dc=1)).wait_recv()
         split_weight([(1, 0), (1, 1), (2, 0), (2, 1)])
@@ -339,26 +380,28 @@
         preact(1, 2, 1)
         pre_grad(1)
         pre_grad(2)
-        for p in range(PIECES // 2):
+        for p in range(EARLY // 2):
             for d in (1, 0):
                 weight_grad(1, 2, 1 - d, p, 1)
-                if p < EARLY // 2:
-                    straight(d, 2 * p).start()
-                    straight(d, 2 * p + 1).start()
+                straight(d, 2 * p).start()
+                straight(d, 2 * p + 1).start()
         for d in range(2):
-            for p in range(PIECES):
+            for p in range(UNITS):
                 unit = wf.at[3, d, piece(p)]
                 remote(unit, unit, gs.at[d, p], gr.at[d, p], me.step(dc=1)).wait_recv()
         split_weight([(3, 0), (3, 1)])
         preact(3, 1, 0)
         preact(3, 1, 1)
         pre_grad(3)
-        for p in range(PIECES // 2):
+        for p in range(EARLY // 2):
             for d in range(2):
                 weight_grad(3, 1, d, p, 1)
-                if p < EARLY // 2:
-                    opposite(d, 2 * p).start()
-                    opposite(d, 2 * p + 1).start()
+                opposite(d, 2 * p).start()
+                opposite(d, 2 * p + 1).start()
+        for s in range(2):
+            weight_grad(0, 3, s, EARLY // 2, PIECES // 2 - EARLY // 2)
+            weight_grad(3, 1, s, EARLY // 2, PIECES // 2 - EARLY // 2)
+            weight_grad(0, 1, s, 0, EARLY // 2)
 
     f32, bf16 = jnp.float32, jnp.bfloat16
     pl.run_scoped(
@@ -426,35 +469,6 @@
                 far[d, :, block(p)] = far[d, :, block(p)] + dw[2 - d, d, :, block(p)]
                 onward(d, p).start()
 
-        input_grad(0)
-        input_grad(1)
-        y_far(1)
-        x_pass(0)
-        x_pass(1)
-        input_grad(2)
-        y_straight(1, 0)
-        input_grad(3)
-        y_straight(1, 1)
-        input_grad(4)
-        x_pass(2)
-        y_pass(1)
-        on_chip(3)
-        input_grad(5)
-        y_far(0)
-        x_pass(3)
-        for p in range(EARLY, PIECES):
-            for d in range(2):
-                opposite(d, p).start()
-        for p in range(EARLY, PIECES):
-            for d in range(2):
-                straight(d, p).start()
-        input_grad(6)
-        y_straight(0, 0)
-        input_grad(7)
-        y_straight(0, 1)
-        on_chip(7)
-        last = remote(acc.at[3, own], xz, s2, r2, me.step(dz=2))
-
         def x_sum(p):
             for d in range(2):
                 straight(d, p).wait_recv()
@@ -478,18 +492,44 @@
                 zin[0, :, block(p)] = dw[0, 1, :, block(p)] + zin[0, :, block(p)]
                 remote(here, zin.at[1, :, block(p)], os_.at[p], qr.at[1, p], me.to_inner).start()
 
+        input_grad(0)
+        input_grad(1)
+        y_far(1)
+        for p in range(EARLY):
+            x_pass(p)
+        for p in range(EARLY, PIECES):
+            for d in range(2):
+                opposite(d, p).start()
+        for p in range(EARLY, PIECES):
+            for d in range(2):
+                straight(d, p).start()
+        input_grad(2)
+        y_straight(1, 0)
         x_sum(0)
+        input_grad(3)
+        y_straight(1, 1)
         x_sum(1)
         z_pass(0)
+        input_grad(4)
+        y_pass(1)
         x_sum(2)
         z_pass(1)
+        on_chip(3)
+        input_grad(5)
+        y_far(0)
         x_sum(3)
         z_pass(2)
-        y_sum(1)
-        last.start()
+        input_grad(6)
+        y_straight(0, 0)
+        input_grad(7)
+        y_straight(0, 1)
+        on_chip(7)
         z_pass(3)
         x_pass(4)
         x_pass(5)
+        y_sum(1)
+        last = remote(acc.at[3, own], xz, s2, r2, me.step(dz=2))
+        last.start()
         y_pass(0)
         x_sum(4)
         z_pass(4)
@@ -523,6 +563,7 @@
             for d in range(2):
                 for copy in (opposite(d, p), straight(d, p), onward(d, p)):
                     copy.wait_send()
+        for p in range(UNITS):
             unit = wt.at[piece(p)]
             remote(unit, unit, zs.at[p], zs.at[p], me.step(dc=1)).wait_send()
 
@@ -534,6 +575,17 @@
                 for s in range(2):
                     remote(unit, unit, xs.at[d, s, p], xs.at[d, s, p], me.step(dc=1)).wait_send()
                 remote(unit, unit, gs.at[d, p], gs.at[d, p], me.step(dc=1)).wait_send()
+        for j in range(4):
+            unit = wt.at[turned]
+            remote(unit, unit, bzs.at[j], bzs.at[j], me.step(dc=1)).wait_send()
+
+            @pl.when(me.inner)
+            def _():
+                remote(unit, unit, bfs.at[j], bfs.at[j], me.step(dc=1)).wait_send()
+
+        for d in range(2):
+            row_out(d).wait_send()
+            row_on(d).wait_send()
         for h in range(2):
             fetch(h).wait_send()
             for d in range(2):
@@ -556,7 +608,7 @@
     r, d = wt.shape
     t = inputs.shape[0]
     hbm = pl.BlockSpec(memory_space=pltpu.HBM)
-    n = PIECES
+    n, u = PIECES, UNITS
     return pl.pallas_call(
         kernel,
         out_shape=(
@@ -564,17 +616,19 @@
             jax.ShapeDtypeStruct((r, t), f32),
             jax.ShapeDtypeStruct((t, d), f32),
             jax.ShapeDtypeStruct((4, 2, r, d), f32),
+            jax.ShapeDtypeStruct((4, r // n, d), f32),
         ),
         in_specs=[hbm] * 3,
-        out_specs=(hbm,) * 4,
+        out_specs=(hbm,) * 5,
         scratch_shapes=[
             vmem((4 * r, 2 * d), bf16), vmem((4 * r, 2 * d), bf16), vmem((4 * r, t), bf16), vmem((4 * r, t), bf16),
             vmem((4, 2, r, d), f32), vmem((2, r, d), f32), vmem((2, 2, r, d), f32), vmem((2, r, d), f32),
             vmem((8, r, t), f32), vmem((2, 2, r, t // 2), f32), vmem((2, 2, r, t), f32), vmem((r, t), f32),
-            dma((n,)), dma((2, n)), dma((n,)), dma((2, 2, n)), dma((2, 2, n)), dma((2, n)), dma((2, n)),
+            dma((u,)), dma((2, u)), dma((u,)), dma((2, 2, u)), dma((2, 2, u)), dma((2, u)), dma((2, u)),
             dma((2,)), dma((2,)), dma((2, 2)), dma((2, 2)), dma((2, 2)), dma((2, 2)), dma((2, 4)), dma((2, 4)), dma((2,)),
             dma((2, n)), dma((2, n)), dma((2, 2, n)), dma((2, 2, n)), dma((n,)), dma((2, n)), dma((n,)),
             dma((8,)), dma((8,)), dma((2, 2)), dma((2, 2)), dma((2, 2, 2)), dma((2, 2, 2)), dma, dma,
+            dma((2,)), dma((2,)), dma((2,)), dma((2,)), dma((4,)), dma((4, 2)), dma((4,)),
         ],
         compiler_params=pltpu.CompilerParams(collective_id=0, has_side_effects=True, vmem_limit_bytes=60 << 20),
     )(inputs, wt, cot)[:2]

time: 205 us -> 202 us (0.985)
  Pallas kernels: 199 us -> 195 us
    pallas_call x1, Pallas kernels: 199 us -> 195 us  [fused(): pl.pallas_call(kernel, out_shape=(jax.ShapeDtypeStruct((r, d), f32), jax....]
where the time goes in v5:
time: 202 us; the launch traced here: 200 us
  Pallas kernels  195 us (97%)
  local copies, waits for them, and re-layouts  4.45 us (2%)
    pallas_call x1, Pallas kernels, fused(): pl.pallas_call(kernel, out_shape=(jax.ShapeDtypeStruct((r, d), f32), jax....  195 us
    unnamed x2, local copies, waits for them, and re-layouts  4.45 us

profile of v5, /device:TPU:32, one launch (start us, length us, event | category | flops | bytes accessed | tf_op | source)
XLA Modules:
  0.0 200.1 jit_solution(16582161803867477583)
XLA Ops:
  0.6 195.0 %shard_map.50 = (f32[192,1536]{1,0:T(8,128)}, f32[192,1024]{1,0:T(8,128)}, f32[1024,1536]{1,0:T(8,128)}, f32[4,2,192,1536]{3,2,1,0:T(8,128)}, f32[4,32,1536]{2,1,0:T(8,128)}) custom-call(f32[1024,1536]{1,0:T(8,128)} %inputs.1, f32[192,1536]{1,0:T(8,128)} %bitcast.4, f32[1024,1536]{1,0:T(8,128)} %cot.1), custom_call_target="tpu_custom_call" | custom-call | tf_op jit(solution)/shard_map/pallas_call | solution.py:612
  195.7 2.1 %copy.7 = f32[1024,192]{0,1:T(8,128)} copy(f32[1024,192]{0,1:T(8,128)} %bitcast.5) | data formatting | bytes 1572864
  197.8 2.4 %copy.8 = f32[1536,192]{0,1:T(8,128)} copy(f32[1536,192]{0,1:T(8,128)} %bitcast.3) | data formatting | bytes 2359296

commit v6 on v5

--- a/solution.py
+++ b/solution.py
@@ -493,8 +493,8 @@
                 remote(here, zin.at[1, :, block(p)], os_.at[p], qr.at[1, p], me.to_inner).start()
 
         input_grad(0)
+        y_far(1)
         input_grad(1)
-        y_far(1)
         for p in range(EARLY):
             x_pass(p)
         for p in range(EARLY, PIECES):
@@ -525,11 +525,11 @@
         y_straight(0, 1)
         on_chip(7)
         z_pass(3)
-        x_pass(4)
-        x_pass(5)
         y_sum(1)
         last = remote(acc.at[3, own], xz, s2, r2, me.step(dz=2))
         last.start()
+        x_pass(4)
+        x_pass(5)
         y_pass(0)
         x_sum(4)
         z_pass(4)

time: 202 us -> 202 us (level)
  no operation moved by 1% of the time
where the time goes in v6:
time: 202 us; the launch traced here: 201 us
  Pallas kernels  196 us (97%)
  local copies, waits for them, and re-layouts  4.45 us (2%)
    pallas_call x1, Pallas kernels, fused(): pl.pallas_call(kernel, out_shape=(jax.ShapeDtypeStruct((r, d), f32), jax....  196 us
    unnamed x2, local copies, waits for them, and re-layouts  4.45 us

profile of v6, /device:TPU:32, one launch (start us, length us, event | category | flops | bytes accessed | tf_op | source)
XLA Modules:
  0.0 201.0 jit_solution(18200471928651278731)
XLA Ops:
  0.6 196.0 %shard_map.50 = (f32[192,1536]{1,0:T(8,128)}, f32[192,1024]{1,0:T(8,128)}, f32[1024,1536]{1,0:T(8,128)}, f32[4,2,192,1536]{3,2,1,0:T(8,128)}, f32[4,32,1536]{2,1,0:T(8,128)}) custom-call(f32[1024,1536]{1,0:T(8,128)} %inputs.1, f32[192,1536]{1,0:T(8,128)} %bitcast.4, f32[1024,1536]{1,0:T(8,128)} %cot.1), custom_call_target="tpu_custom_call" | custom-call | tf_op jit(solution)/shard_map/pallas_call | solution.py:612
  196.6 2.1 %copy.7 = f32[1024,192]{0,1:T(8,128)} copy(f32[1024,192]{0,1:T(8,128)} %bitcast.5) | data formatting | bytes 1572864
  198.7 2.4 %copy.8 = f32[1536,192]{0,1:T(8,128)} copy(f32[1536,192]{0,1:T(8,128)} %bitcast.3) | data formatting | bytes 2359296
